TPU v7x, 32 devices: a whole 2x2x4 slice. The times are simulated.
32 devices in a mesh: seq: 4 (over y, core), ctx: 8 (over z, x).
Axes of the slice: x: 2, y: 2, z: 4, core: 2. Of those that a mesh axis runs over, the one named last changes fastest.
Arguments:
- tokens: bfloat16 [4, 1024, 2048], P('seq', 'ctx'), may hold values from -6 to 6
- cotangent: bfloat16 [4, 1024, 2048], P('seq', 'ctx'), may hold values from -6 to 6
- gain_attn: bfloat16 [2048], P(('seq', 'ctx')), may hold values from 0.099609375 to 1.8984375
- w_query: bfloat16 [2048, 2048], P(('seq', 'ctx')), may hold values from -0.125 to 0.125
- w_key: bfloat16 [2048, 1024], P(('seq', 'ctx')), may hold values from -0.125 to 0.125
- w_value: bfloat16 [2048, 1024], P(('seq', 'ctx')), may hold values from -0.125 to 0.125
- w_out: bfloat16 [2048, 2048], P(('seq', 'ctx')), may hold values from -1 to 1
- gain_mlp: bfloat16 [2048], P(('seq', 'ctx')), may hold values from 0.099609375 to 1.8984375
- w_gate: bfloat16 [2048, 8192], P(('seq', 'ctx')), may hold values from -0.125 to 0.125
- w_up: bfloat16 [2048, 8192], P(('seq', 'ctx')), may hold values from -0.125 to 0.125
- w_down: bfloat16 [8192, 2048], P(('seq', 'ctx')), may hold values from -0.0625 to 0.0625
- pair_order: int32 [4, 8], P('seq'), may hold values from 0 to 7, each once within a row
- segments: int32 [4, 1024], P('seq'), may hold values from 0 to 3, never falling along the last dimension, each value on 1 to 512 neighbouring positions
Outputs:
- output: bfloat16 [4, 1024, 2048], P('seq', 'ctx')
- grad_tokens: float32 [4, 1024, 2048], P('seq', 'ctx')
- grad_gain_attn: float32 [2048], P(('seq', 'ctx'))
- grad_w_query: float32 [2048, 2048], P(('seq', 'ctx'))
- grad_w_key: float32 [2048, 1024], P(('seq', 'ctx'))
- grad_w_value: float32 [2048, 1024], P(('seq', 'ctx'))
- grad_w_out: float32 [2048, 2048], P(('seq', 'ctx'))
- grad_gain_mlp: float32 [2048], P(('seq', 'ctx'))
- grad_w_gate: float32 [2048, 8192], P(('seq', 'ctx'))
- grad_w_up: float32 [2048, 8192], P(('seq', 'ctx'))
- grad_w_down: float32 [8192, 2048], P(('seq', 'ctx'))
Inputs may be any that keep to these rules, and one draw needn't show every extreme that they name: `segments`: along a sequence the document numbers never fall; each document has 1 to 512 tokens. `pair_order`: each row holds every number of 0 to 7 once.
All inputs are finite; a program needn't handle non-finite values.
Results may differ from a plain program's by a relative error of at most 0.022.
Values may be sent and summed in bfloat16 or wider, within the bound.
A program may use at most 448 MiB of HBM per device.

v0:
```python
import functools
import math

import jax
import jax.numpy as jnp
import numpy as np
from jax import lax
from jax.experimental import pallas as pl
from jax.experimental.pallas import tpu as pltpu
from jax.sharding import PartitionSpec as P

H = 8
KVH = 4
HDIM = 256
DOCS = 4


EPSILON = 1e-06
THETA = 1000042.0
NEG_FILL = -1e30


def slot_positions(pair_row, half_rows, pair_count):
    offsets = jnp.arange(half_rows, dtype=jnp.int32)
    low_slots = pair_row[:, None] * half_rows + offsets[None, :]
    high_slots = (2 * pair_count - 1 - pair_row)[:, None] * half_rows + offsets[None, :]
    return jnp.concatenate([low_slots, high_slots], axis=1).reshape(-1)


def rotary_tables(positions, head_dim):
    half_dim = head_dim // 2
    frequency = THETA ** (-(jnp.arange(half_dim, dtype=jnp.float32) * 2.0 / head_dim))
    angles = positions.astype(jnp.float32)[:, None] * frequency[None, :]
    return (jnp.cos(angles)[:, None, :], jnp.sin(angles)[:, None, :])


def rotary(tensor, table_cos, table_sin):
    half_dim = tensor.shape[-1] // 2
    lead_half = tensor[..., :half_dim]
    tail_half = tensor[..., half_dim:]
    return jnp.concatenate(
        [
            lead_half * table_cos - tail_half * table_sin,
            tail_half * table_cos + lead_half * table_sin,
        ],
        axis=-1,
    )


def rms_scale(tensor):
    return lax.rsqrt(jnp.mean(tensor * tensor, axis=-1, keepdims=True) + EPSILON)


def rms_backward(tensor, scale_rows, gain_full, grad_rows):
    weighted = gain_full * grad_rows
    inner_mean = jnp.mean(weighted * tensor, axis=-1, keepdims=True)
    return scale_rows * weighted - tensor * (scale_rows * scale_rows * scale_rows) * inner_mean


def contract_rows(first_mat, second_mat):
    return lax.dot_general(
        first_mat, second_mat, (((0,), (0,)), ((), ())), preferred_element_type=jnp.float32
    )


def contract_cols(first_mat, second_mat):
    return lax.dot_general(
        first_mat, second_mat, (((1,), (1,)), ((), ())), preferred_element_type=jnp.float32
    )


def attention_weights(gain_attn, gain_mlp, w_query, w_key, w_value, w_out):
    return (
        lax.all_gather(gain_attn, ("seq", "ctx"), axis=0, tiled=True),
        lax.all_gather(gain_mlp, ("seq", "ctx"), axis=0, tiled=True),
        lax.all_gather(w_query, ("seq", "ctx"), axis=0, tiled=True),
        lax.all_gather(w_key, ("seq", "ctx"), axis=0, tiled=True),
        lax.all_gather(w_value, ("seq", "ctx"), axis=0, tiled=True),
        lax.all_gather(w_out, ("seq", "ctx"), axis=0, tiled=True),
    )


def mlp_weights(w_gate, w_up, w_down):
    return (
        lax.all_gather(w_gate, ("seq", "ctx"), axis=0, tiled=True),
        lax.all_gather(w_up, ("seq", "ctx"), axis=0, tiled=True),
        lax.all_gather(w_down, ("seq", "ctx"), axis=0, tiled=True),
    )


def reduce_grads(grad_one, grad_two, grad_three):
    seq_count = lax.axis_size("seq")
    grad_one = grad_one.reshape((seq_count, grad_one.shape[0] // seq_count) + grad_one.shape[1:])
    grad_two = grad_two.reshape((seq_count, grad_two.shape[0] // seq_count) + grad_two.shape[1:])
    grad_three = grad_three.reshape(
        (seq_count, grad_three.shape[0] // seq_count) + grad_three.shape[1:]
    )
    grad_one, grad_two, grad_three = (
        lax.psum_scatter(
            grad_one.astype(jnp.bfloat16), "ctx", scatter_dimension=1, tiled=True
        ).astype(jnp.float32),
        lax.psum_scatter(
            grad_two.astype(jnp.bfloat16), "ctx", scatter_dimension=1, tiled=True
        ).astype(jnp.float32),
        lax.psum_scatter(
            grad_three.astype(jnp.bfloat16), "ctx", scatter_dimension=1, tiled=True
        ).astype(jnp.float32),
    )
    grad_one, grad_two, grad_three = (
        lax.psum_scatter(
            grad_one.astype(jnp.bfloat16), "seq", scatter_dimension=0, tiled=True
        ).astype(jnp.float32),
        lax.psum_scatter(
            grad_two.astype(jnp.bfloat16), "seq", scatter_dimension=0, tiled=True
        ).astype(jnp.float32),
        lax.psum_scatter(
            grad_three.astype(jnp.bfloat16), "seq", scatter_dimension=0, tiled=True
        ).astype(jnp.float32),
    )
    return (grad_one[0], grad_two[0], grad_three[0])


def general_device(
    tokens,
    cotangent,
    gain_attn,
    w_query,
    w_key,
    w_value,
    w_out,
    gain_mlp,
    w_gate,
    w_up,
    w_down,
    pair_order,
    segments,
):
    pair_count = lax.axis_size("ctx")
    my_index = lax.axis_index("ctx")
    row_count = tokens.shape[1]
    half_rows = row_count // 2
    seq_len = segments.shape[1]
    head_groups = H // KVH
    score_scale = HDIM ** (-0.5)
    key_rows = math.gcd(seq_len, 512)
    key_steps = seq_len // key_rows
    key_pos = slot_positions(pair_order[0], half_rows, pair_count)
    key_doc = jnp.take(segments[0], key_pos)
    query_pos = lax.dynamic_slice_in_dim(key_pos, my_index * row_count, row_count)
    query_doc = lax.dynamic_slice_in_dim(key_doc, my_index * row_count, row_count)
    rot_cos, rot_sin = rotary_tables(query_pos, HDIM)
    gain_one, gain_two, query_w, key_w, value_w, out_w = attention_weights(
        gain_attn, gain_mlp, w_query, w_key, w_value, w_out
    )
    gain_one = gain_one.astype(jnp.float32)
    gain_two = gain_two.astype(jnp.float32)
    inputs = tokens[0].astype(jnp.float32)
    scale_one = rms_scale(inputs)
    normed = (inputs * scale_one * gain_one).astype(jnp.bfloat16)
    query_proj = jnp.dot(normed, query_w, preferred_element_type=jnp.float32).reshape(
        row_count, H, HDIM
    )
    key_proj = jnp.dot(normed, key_w, preferred_element_type=jnp.float32).reshape(
        row_count, KVH, HDIM
    )
    value_proj = jnp.dot(normed, value_w, preferred_element_type=jnp.float32)
    query_rot = (
        rotary(query_proj, rot_cos, rot_sin)
        .astype(jnp.bfloat16)
        .reshape(row_count, KVH, head_groups, HDIM)
    )
    key_rot = rotary(key_proj, rot_cos, rot_sin).astype(jnp.bfloat16).reshape(row_count, KVH * HDIM)
    value_low = value_proj.astype(jnp.bfloat16)
    key_width = key_rot.shape[1]
    key_all, value_all = (
        lax.all_gather(key_rot, "ctx", axis=0, tiled=True),
        lax.all_gather(value_low, "ctx", axis=0, tiled=True),
    )
    pos_blocks = key_pos.reshape(key_steps, key_rows)
    doc_blocks = key_doc.reshape(key_steps, key_rows)

    def scores_of(key_blk, pos_blk, doc_blk):
        key_heads = key_blk.reshape(key_rows, KVH, HDIM)
        raw_scores = (
            jnp.einsum("qkgd,tkd->kgqt", query_rot, key_heads, preferred_element_type=jnp.float32)
            * score_scale
        )
        visible = (doc_blk[None, :] == query_doc[:, None]) & (
            pos_blk[None, :] <= query_pos[:, None]
        )
        return (raw_scores, visible[None, None])

    def first_pass(carried, step_data):
        running_top, running_sum = carried
        key_blk, pos_blk, doc_blk = step_data
        raw_scores, visible = scores_of(key_blk, pos_blk, doc_blk)
        masked = jnp.where(visible, raw_scores, NEG_FILL)
        new_top = jnp.maximum(running_top, jnp.max(masked, axis=-1))
        added = jnp.sum(jnp.where(visible, jnp.exp(masked - new_top[..., None]), 0.0), axis=-1)
        return ((new_top, running_sum * jnp.exp(running_top - new_top) + added), None)

    start_top = jnp.full((KVH, head_groups, row_count), NEG_FILL, jnp.float32)
    start_sum = jnp.zeros((KVH, head_groups, row_count), jnp.float32)
    key_stack = key_all.reshape(key_steps, key_rows, key_width)
    value_stack = value_all.reshape(key_steps, key_rows, key_width)
    (final_top, final_sum), _ = lax.scan(
        first_pass, (start_top, start_sum), (key_stack, pos_blocks, doc_blocks)
    )
    log_total = final_top + jnp.log(final_sum)

    def second_pass(carried, step_data):
        acc_out, acc_rest = carried
        key_blk, value_blk, pos_blk, doc_blk = step_data
        raw_scores, visible = scores_of(key_blk, pos_blk, doc_blk)
        prob_full = jnp.where(visible, jnp.exp(raw_scores - log_total[..., None]), 0.0)
        prob_low = prob_full.astype(jnp.bfloat16)
        prob_rest = (prob_full - prob_low.astype(jnp.float32)).astype(jnp.bfloat16)
        value_heads = value_blk.reshape(key_rows, KVH, HDIM)
        acc_out = acc_out + jnp.einsum(
            "kgqt,tkd->qkgd", prob_low, value_heads, preferred_element_type=jnp.float32
        )
        acc_rest = acc_rest + jnp.einsum(
            "kgqt,tkd->qkgd", prob_rest, value_heads, preferred_element_type=jnp.float32
        )
        return ((acc_out, acc_rest), None)

    start_acc = jnp.zeros((row_count, KVH, head_groups, HDIM), jnp.float32)
    (attended, attended_rest), _ = lax.scan(
        second_pass, (start_acc, start_acc), (key_stack, value_stack, pos_blocks, doc_blocks)
    )
    exact_out = attended + attended_rest
    out_low = attended.reshape(row_count, H * HDIM).astype(jnp.bfloat16)
    hidden = inputs + jnp.dot(out_low, out_w, preferred_element_type=jnp.float32)
    scale_two = rms_scale(hidden)
    normed_two = (hidden * scale_two * gain_two).astype(jnp.bfloat16)
    grad_out = cotangent[0]
    gate_w, up_w, down_w = mlp_weights(w_gate, w_up, w_down)
    gate_proj = jnp.dot(normed_two, gate_w, preferred_element_type=jnp.float32)
    up_proj = jnp.dot(normed_two, up_w, preferred_element_type=jnp.float32)
    gate_sig = jax.nn.sigmoid(gate_proj)
    active = gate_proj * gate_sig
    middle = (active * up_proj).astype(jnp.bfloat16)
    result = hidden + jnp.dot(middle, down_w, preferred_element_type=jnp.float32)
    output = result.astype(jnp.bfloat16)[None]
    gate_w, up_w, down_w = mlp_weights(w_gate, w_up, w_down)
    grad_mid = contract_cols(grad_out, down_w)
    grad_gate = (grad_mid * up_proj * gate_sig * (1.0 + gate_proj * (1.0 - gate_sig))).astype(
        jnp.bfloat16
    )
    grad_up = (grad_mid * active).astype(jnp.bfloat16)
    grad_norm_two = contract_cols(grad_gate, gate_w) + contract_cols(grad_up, up_w)
    grad_gain_two = jnp.sum(grad_norm_two * hidden * scale_two, axis=0)
    grad_hidden = grad_out.astype(jnp.float32) + rms_backward(
        hidden, scale_two, gain_two, grad_norm_two
    )
    grad_w_gate = contract_rows(normed_two, grad_gate)
    grad_w_up = contract_rows(normed_two, grad_up)
    shard_gain_two, shard_gate, shard_up = reduce_grads(grad_gain_two, grad_w_gate, grad_w_up)
    gain_one, gain_two, query_w, key_w, value_w, out_w = attention_weights(
        gain_attn, gain_mlp, w_query, w_key, w_value, w_out
    )
    gain_one = gain_one.astype(jnp.float32)
    grad_branch = grad_hidden.astype(jnp.bfloat16)
    grad_w_out = contract_rows(out_low, grad_branch)
    grad_att = (
        contract_cols(grad_branch, out_w)
        .astype(jnp.bfloat16)
        .reshape(row_count, KVH, head_groups, HDIM)
    )
    row_delta = jnp.transpose(jnp.sum(grad_att.astype(jnp.float32) * exact_out, axis=-1), (1, 2, 0))
    key_back, value_back = (key_all, value_all)

    def backward_step(grad_query, step_data):
        key_blk, value_blk, pos_blk, doc_blk = step_data
        raw_scores, visible = scores_of(key_blk, pos_blk, doc_blk)
        prob_full = jnp.where(visible, jnp.exp(raw_scores - log_total[..., None]), 0.0)
        prob_low = prob_full.astype(jnp.bfloat16)
        key_heads = key_blk.reshape(key_rows, KVH, HDIM)
        value_heads = value_blk.reshape(key_rows, KVH, HDIM)
        grad_value_blk = jnp.einsum(
            "kgqt,qkgd->tkd", prob_low, grad_att, preferred_element_type=jnp.float32
        )
        grad_probs = jnp.einsum(
            "qkgd,tkd->kgqt", grad_att, value_heads, preferred_element_type=jnp.float32
        )
        grad_scores = (prob_full * (grad_probs - row_delta[..., None])).astype(jnp.bfloat16)
        grad_query = (
            grad_query
            + jnp.einsum(
                "kgqt,tkd->qkgd", grad_scores, key_heads, preferred_element_type=jnp.float32
            )
            * score_scale
        )
        grad_key_blk = (
            jnp.einsum("kgqt,qkgd->tkd", grad_scores, query_rot, preferred_element_type=jnp.float32)
            * score_scale
        )
        return (
            grad_query,
            (
                grad_key_blk.reshape(key_rows, key_width),
                grad_value_blk.reshape(key_rows, key_width),
            ),
        )

    back_keys = key_back.reshape(key_steps, key_rows, key_width)
    back_values = value_back.reshape(key_steps, key_rows, key_width)
    grad_query, (grad_key_steps, grad_value_steps) = lax.scan(
        backward_step, start_acc, (back_keys, back_values, pos_blocks, doc_blocks)
    )
    grad_key_all = grad_key_steps.reshape(seq_len, key_width)
    grad_value_all = grad_value_steps.reshape(seq_len, key_width)
    grad_key_own, grad_value_own = (
        lax.psum_scatter(
            grad_key_all.astype(jnp.bfloat16), "ctx", scatter_dimension=0, tiled=True
        ).astype(jnp.float32),
        lax.psum_scatter(
            grad_value_all.astype(jnp.bfloat16), "ctx", scatter_dimension=0, tiled=True
        ).astype(jnp.float32),
    )
    grad_query = (
        rotary(grad_query.reshape(row_count, H, HDIM), rot_cos, -rot_sin)
        .astype(jnp.bfloat16)
        .reshape(row_count, H * HDIM)
    )
    grad_key = (
        rotary(grad_key_own.reshape(row_count, KVH, HDIM), rot_cos, -rot_sin)
        .astype(jnp.bfloat16)
        .reshape(row_count, key_width)
    )
    grad_value = grad_value_own.astype(jnp.bfloat16)
    grad_w_query = contract_rows(normed, grad_query)
    grad_w_key = contract_rows(normed, grad_key)
    grad_w_value = contract_rows(normed, grad_value)
    grad_normed = (
        contract_cols(grad_query, query_w)
        + contract_cols(grad_key, key_w)
        + contract_cols(grad_value, value_w)
    )
    grad_gain_one = jnp.sum(grad_normed * inputs * scale_one, axis=0)
    grad_tokens = grad_hidden + rms_backward(inputs, scale_one, gain_one, grad_normed)
    grad_w_down = contract_rows(middle, grad_out)
    shard_gain_one, shard_out, shard_down = reduce_grads(grad_gain_one, grad_w_out, grad_w_down)
    shard_query, shard_key, shard_value = reduce_grads(grad_w_query, grad_w_key, grad_w_value)
    return (
        output,
        grad_tokens[None],
        shard_gain_one,
        shard_query,
        shard_key,
        shard_value,
        shard_out,
        shard_gain_two,
        shard_gate,
        shard_up,
        shard_down,
    )


MESH = pl.DeviceIdType.MESH
VMEM = pltpu.VMEM
RING = 8
SEQ = 4


class Place:
    def __init__(self):
        self.c = lax.axis_index("ctx")
        self.s = lax.axis_index("seq")
        self.z, self.x = self.c // 2, lax.rem(self.c, 2)
        self.p = self.z + self.x * (7 - 2 * self.z)
        self.up, self.down = {"ctx": self.c + 2}, {"ctx": self.c - 2}
        self.side = {"ctx": self.c + 1 - 2 * self.x}
        self.right = {"ctx": self.at(1)}
        self.left = {"ctx": self.at(-1)}
        self.s_core = self.s + 1 - 2 * lax.rem(self.s, 2)
        self.s_far = lax.rem(self.s + 2, 4)
        self.s_both = 3 - self.s
        self.core_peer = {"seq": self.s_core}
        self.far_peer = {"seq": self.s_far}

    def at(self, offset):
        q = lax.rem(self.p + offset + 2 * RING, RING)
        return 2 * q + (q // 4) * (15 - 4 * q)

    def peers(self):
        return [{"ctx": lax.rem(self.c + k, RING)} for k in range(1, RING)]


def greet(devices):
    barrier = pltpu.get_barrier_semaphore()
    for device in devices:
        pl.semaphore_signal(barrier, inc=1, device_id=device, device_id_type=MESH)
    pl.semaphore_wait(barrier, len(devices))


def remote(src, dst, send_sem, recv_sem, device):
    return pltpu.make_async_remote_copy(
        src_ref=src, dst_ref=dst, send_sem=send_sem, recv_sem=recv_sem, device_id=device, device_id_type=MESH
    )


def arrived(ref, sems, index, device):
    remote(ref, ref, sems[0].at[index], sems[1].at[index], device).wait_recv()


def together(*flows):
    live = list(flows)
    while live:
        live = [flow for flow in live if next(flow, "end") != "end"]


def ring_sems():
    return [pltpu.SemaphoreType.DMA((2, RING // 2, 2))] * 2


def slot(offset):
    return 0 if offset == 0 else min(RING - 1, 2 * offset if offset > 0 else -2 * offset - 1)


class Rows:
    def __init__(self, ref, rows):
        self.ref, self.rows = ref, rows

    def here(self, offset):
        return self.ref.at[pl.ds(slot(offset) * self.rows, self.rows)]

    def there(self, offset, d):
        return self.here(offset - 1 if d == 0 else offset + 1)


class Owners:
    def __init__(self, ref, place):
        self.ref, self.place = ref, place

    def here(self, offset):
        return self.ref.at[self.place.at(offset)]

    def there(self, offset, d):
        return self.here(offset)


def ring_gather(own, blocks, sems, place):
    half = own.shape[0] // 2
    steps = RING // 2
    sent = []

    def part(ref, j):
        return ref.at[pl.ds(j * half, half)]

    def wait_for(d, s, j):
        offset = -(s + 1) if d == 0 else s + 1
        arrived(part(blocks.here(offset), j), sems, (d, s, j), place.right if d == 0 else place.left)

    for s in range(steps):
        for j in range(2):
            for d in range(2):
                if s == steps - 1 and j != d:
                    continue
                if s > 0:
                    wait_for(d, s - 1, j)
                offset = -s if d == 0 else s
                copy = remote(
                    part(own if s == 0 else blocks.here(offset), j),
                    part(blocks.there(offset, d), j),
                    sems[0].at[d, s, j],
                    sems[1].at[d, s, j],
                    place.right if d == 0 else place.left,
                )
                copy.start()
                sent.append(copy)
            yield
    for d in range(2):
        wait_for(d, steps - 2, 1 - d)
    yield
    for d in range(2):
        wait_for(d, steps - 1, d)
    yield
    for copy in sent:
        copy.wait_send()


class RingSum:
    def __init__(self, slots, sems, place):
        self.slots, self.sems, self.sent = slots, sems, []
        self.sides = (place.right, place.left)
        self.half = slots.shape[2] // 2

    def rows(self, ref, j):
        return ref.at[pl.ds(j * self.half, self.half)]

    def send(self, d, s, j, source):
        to = self.rows(self.slots.at[d, s], j)
        copy = remote(source, to, self.sems[0].at[d, s, j], self.sems[1].at[d, s, j], self.sides[d])
        copy.start()
        self.sent.append(copy)

    def held(self, d, s, j):
        ref = self.rows(self.slots.at[d, s], j)
        arrived(ref, self.sems, (d, s, j), self.sides[d])
        return ref

    def first(self, part):
        for d in range(2):
            self.send(d, 0, d, self.rows(part, d))

    def relay(self, s, parts):
        for j in range(2):
            for d in range(2):
                source = self.rows(parts[d], j)
                if s > 1 or j == d:
                    held = self.held(d, s - 1, j)
                    add_into(held, source)
                    source = held
                self.send(d, s, j, source)

    def last(self, part, out):
        for j in range(2):
            held = [self.held(d, RING // 2 - 1, j) for d in range(2)]
            sum_of_three(self.rows(out, j), self.rows(part, j), *held)

    def end(self):
        for copy in self.sent:
            copy.wait_send()


def ring_scatter(blocks, out, slots, sems, place):
    ring = RingSum(slots, sems, place)
    ring.first(blocks.here(RING // 2))
    yield
    for s in range(1, RING // 2):
        k = RING // 2 - s
        ring.relay(s, (blocks.here(k), blocks.here(-k)))
        yield
    ring.last(blocks.here(0), out)
    ring.end()
    yield


def pair_sems():
    return [pltpu.SemaphoreType.DMA((RING,))] * 2


OFFSETS = (1, -1, 2, -2, 3, -3, 4)


def exchange(pieces, here, sems, place, group=RING):
    for i in range(0, len(OFFSETS), group):
        for k in OFFSETS[i : i + group]:
            at = slot(k)
            for src, dst in pieces(k):
                remote(src, dst, sems[0].at[at], sems[1].at[at], {"ctx": place.at(k)}).start()
        yield
    for k in OFFSETS:
        arrived(here(k), sems, RING - 1 if k == RING // 2 else slot(-k), {"ctx": place.at(k)})
    for k in OFFSETS:
        remote(here(k), here(k), sems[0].at[slot(k)], sems[1].at[slot(k)], {"ctx": place.at(k)}).wait_send()
    yield


def by_owner(src, dst, sems, place, group=RING):
    return exchange(lambda k: [(src.at[place.at(k)], dst.at[place.c])], lambda k: dst.at[place.at(k)], sems, place, group)


def block_at(i, size):
    return pl.ds(pl.multiple_of(i * size, size), size)


class ByOwner:
    def __init__(self, ref, rows):
        self.ref, self.rows = ref, rows

    def owner(self, c, side=None):
        return self.ref.at[block_at(c, self.rows)]


class ByArrival:
    def __init__(self, ref, rows, place):
        self.ref, self.rows, self.place = ref, rows, place

    def owner(self, c, side="here"):
        far = {"here": 0, "up": 2, "down": -2, "side": 1 - 2 * self.place.x}[side]
        mine = self.place.c + far
        z, x = mine // 2, lax.rem(mine, 2)
        p = z + x * (7 - 2 * z)
        z, x = c // 2, lax.rem(c, 2)
        k = lax.rem(z + x * (7 - 2 * z) - p + 2 * RING, RING)
        late = jnp.where(k == RING // 2, RING - 1, 2 * (RING - k) - 1)
        return self.ref.at[block_at(jnp.where(k < RING // 2, 2 * k, late), self.rows)]


def grid_sems():
    return [pltpu.SemaphoreType.DMA((2, 3))] * 2 + [pltpu.SemaphoreType.DMA((4,))] * 2


def grid_gather(own, blocks, sems, place):
    z_sems, x_sems = sems[:2], sems[2:]
    z, x = place.z, place.x
    sent = []

    def send(when, src, c, side, pair, index, device):
        copy = remote(src, blocks.owner(c, side), pair[0].at[index], pair[1].at[index], device)
        pl.when(when)(copy.start)
        sent.append((when, copy))

    def across(when, src, line):
        send(when, src, 2 * line + x, "side", x_sems, line, place.side)

    send(z < 3, own, place.c, "up", z_sems, (0, 0), place.up)
    send(z > 0, own, place.c, "down", z_sems, (1, 0), place.down)
    across(z >= 0, own, z)
    yield
    for hop in range(1, 4):
        for d, (line, here, further) in enumerate(((z - hop, z >= hop, z < 3), (z + hop, z <= 3 - hop, z > 0))):
            index = 2 * line + x
            ref = blocks.owner(jnp.clip(index, 0, RING - 1))
            device = (place.down, place.up)[d]

            @pl.when(here)
            def _():
                arrived(ref, z_sems, (d, hop - 1), device)

            if hop < 3:
                send(here & further, ref, jnp.clip(index, 0, RING - 1), ("up", "down")[d], z_sems, (d, hop), (place.up, place.down)[d])
            across_line = jnp.clip(line, 0, 3)
            send(here, ref, 2 * across_line + x, "side", x_sems, across_line, place.side)
        yield
    for line in range(4):
        arrived(blocks.owner(2 * line + 1 - x), x_sems, line, place.side)
    for when, copy in sent:
        pl.when(when)(copy.wait_send)
    yield


def grid_sum_sems():
    return [pltpu.SemaphoreType.DMA((4,))] * 2 + [pltpu.SemaphoreType.DMA((2, 4))] * 2


class GridSum:
    def __init__(self, part, over, line, sems, place):
        self.part, self.over, self.line, self.place = part, over, line, place
        self.x_sems, self.z_sems = sems[:2], sems[2:]
        self.rows = over.shape[1]
        self.sent = []

    def plane(self, i):
        z = self.place.z
        inner = jnp.where((z == 1) | (z == 2), 1, 0)
        plain, mid = (3, 2, 1, 0)[i], (3, 0, 2, 1)[i]
        order = plain + inner * (mid - plain)
        return jnp.where(z < 2, order, 3 - order)

    def send(self, when, src, dst, pair, index, device):
        copy = remote(src, dst, pair[0].at[index], pair[1].at[index], device)
        pl.when(when)(copy.start)
        self.sent.append((when, copy))

    def mine(self, z, x):
        return self.part.at[block_at(2 * z + x, self.rows)]

    def across(self, i):
        z = self.plane(i)
        self.send(self.place.z >= 0, self.mine(z, 1 - self.place.x), self.over.at[z], self.x_sems, z, self.place.side)

    def along(self, i):
        z, me = self.plane(i), self.place.z
        held = self.over.at[z]
        arrived(held, self.x_sems, z, self.place.side)
        add_into(held, self.mine(z, self.place.x))
        for d, (when, more, source, device) in enumerate(
            (
                (z > me, me > 0, self.place.down, self.place.up),
                (z < me, me < 3, self.place.up, self.place.down),
            )
        ):

            @pl.when(when & more)
            def _():
                arrived(self.line.at[d, z], self.z_sems, (d, z), source)
                add_into(held, self.line.at[d, z])

            self.send(when, held, self.line.at[d, z], self.z_sems, (d, z), device)

    def last(self, out):
        z = self.place.z
        held = self.over.at[z]
        arrived(held, self.x_sems, z, self.place.side)
        add_to(out, held, self.mine(z, self.place.x))
        for d, (when, source) in enumerate(((z > 0, self.place.down), (z < 3, self.place.up))):

            @pl.when(when)
            def _():
                arrived(self.line.at[d, z], self.z_sems, (d, z), source)
                add_to(out, out, self.line.at[d, z])

    def end(self):
        for when, copy in self.sent:
            pl.when(when)(copy.wait_send)


def pairs_of(sems):
    return [sems[i : i + 2] for i in range(0, len(sems), 2)]


def seq_sems():
    return [pltpu.SemaphoreType.DMA((3,))] * 2


def seq_gather(own, buf, sems, place):
    first = remote(own, buf.at[place.s], sems[0].at[0], sems[1].at[0], place.far_peer)
    second = remote(own, buf.at[place.s], sems[0].at[1], sems[1].at[1], place.core_peer)
    first.start()
    second.start()
    yield
    arrived(buf.at[place.s_far], sems, 0, place.far_peer)
    third = remote(buf.at[place.s_far], buf.at[place.s_far], sems[0].at[2], sems[1].at[2], place.core_peer)
    third.start()
    yield
    arrived(buf.at[place.s_core], sems, 1, place.core_peer)
    arrived(buf.at[place.s_both], sems, 2, place.core_peer)
    for copy in (first, second, third):
        copy.wait_send()
    yield


def sum_of_three(dst, *terms):
    step = math.gcd(dst.shape[0], 16)

    @pl.loop(0, dst.shape[0] // step)
    def _(i):
        at = pl.ds(pl.multiple_of(i * step, step), step)
        one, two, three = (term[at].astype(jnp.float32) for term in terms)
        dst[at] = one + two + three


def add_to(dst, one, two):
    step = math.gcd(dst.shape[0], 16)

    @pl.loop(0, dst.shape[0] // step)
    def _(i):
        at = pl.ds(pl.multiple_of(i * step, step), step)
        dst[at] = one[at].astype(jnp.float32) + two[at].astype(jnp.float32)


def add_into(dst, other):
    rows = dst.shape[0]
    step = math.gcd(rows, 16)

    @pl.loop(0, rows // step)
    def _(i):
        at = pl.ds(pl.multiple_of(i * step, step), step)
        dst[at] = (dst[at].astype(jnp.float32) + other[at].astype(jnp.float32)).astype(dst.dtype)


class SeqSum:
    def __init__(self, grad, block, near, far, sems, place):
        self.grad, self.block, self.near_ref, self.far, self.sems, self.place = grad, block, near, far, sems, place
        self.low, self.row = lax.rem(place.s, 2), place.s // 2
        self.sent = []

    def send(self, src, dst, i, device):
        copy = remote(src, dst, self.sems[0].at[i], self.sems[1].at[i], device)
        copy.start()
        self.sent.append(copy)

    def near(self, i):
        r = (1 - self.row, self.row)[i]
        self.grad(r * 2 + 1 - self.low, self.block.at[i], False)
        self.send(self.block.at[i], self.near_ref.at[i], i, self.place.core_peer)

    def across(self):
        arrived(self.near_ref.at[0], self.sems, 0, self.place.core_peer)
        self.grad((1 - self.row) * 2 + self.low, self.near_ref.at[0], True)
        self.send(self.near_ref.at[0], self.far, 2, self.place.far_peer)

    def own(self):
        arrived(self.near_ref.at[1], self.sems, 1, self.place.core_peer)
        self.grad(self.row * 2 + self.low, self.near_ref.at[1], True)

    def last(self):
        arrived(self.far, self.sems, 2, self.place.far_peer)
        add_into(self.far, self.near_ref.at[1])

    def end(self):
        for copy in self.sent:
            copy.wait_send()


def call(body, outs, args, spaces, out_spaces, scratch, ident):
    return pl.pallas_call(
        body,
        out_shape=outs,
        in_specs=[pl.BlockSpec(memory_space=space) for space in spaces],
        out_specs=[pl.BlockSpec(memory_space=space) for space in out_spaces],
        scratch_shapes=scratch,
        compiler_params=pltpu.CompilerParams(
            collective_id=ident, has_side_effects=True, vmem_limit_bytes=63 * 1024 * 1024
        ),
    )(*args)


def shaped(shape, dtype=jnp.bfloat16):
    return jax.ShapeDtypeStruct(shape, dtype)


def dot(a, b, at=(1, 0)):
    return lax.dot_general(a, b, (((at[0],), (at[1],)), ((), ())), preferred_element_type=jnp.float32)


def chunks(total, size, body):
    @pl.loop(0, total // size)
    def _(i):
        body(pl.ds(pl.multiple_of(i * size, size), size))


def turned(t, cos, sin, sign):
    half = t.shape[1] // 2
    a, b = t[:, :half], t[:, half:]
    return jnp.concatenate([a * cos - sign * b * sin, b * cos + sign * a * sin], axis=-1)


def probabilities(q, k, pos_rows, start_rows, pos_cols):
    scores = dot(q, k, (1, 1)) * HDIM ** (-0.5)
    visible = (pos_cols >= start_rows) & (pos_cols <= pos_rows)
    scores = jnp.where(visible, scores, NEG_FILL)
    weight = jnp.exp(scores - jnp.max(scores, axis=-1, keepdims=True))
    return weight / jnp.sum(weight, axis=-1, keepdims=True)


def place_rows(pairs, segments, block_cos, block_sin, row_cos, row_sin, cos, sin, pos_rows, start_rows, pos_cols):
    f32 = jnp.float32
    half = row_cos.shape[0]
    bounds = [
        jnp.sum(jnp.where(segments[...] < d, 1.0, 0.0).astype(f32), axis=1, keepdims=True) for d in range(1, DOCS)
    ]
    numbers = lax.broadcasted_iota(jnp.int32, block_cos.shape, 0)
    for c in range(RING):
        blocks = (pairs[0, c], 2 * RING - 1 - pairs[0, c])
        lanes = lax.broadcasted_iota(jnp.int32, (1, 2 * half), 1)
        low = blocks[0] * half + lanes
        pos_cols[:, pl.ds(c * 2 * half, 2 * half)] = jnp.where(lanes < half, low, blocks[1] * half + lanes - half).astype(f32)
        for j, block in enumerate(blocks):
            at = pl.ds((2 * c + j) * half, half)
            near_cos = jnp.sum(jnp.where(numbers == block, block_cos[...], 0.0), axis=0, keepdims=True)
            near_sin = jnp.sum(jnp.where(numbers == block, block_sin[...], 0.0), axis=0, keepdims=True)
            cos[at, :] = near_cos * row_cos[...] - near_sin * row_sin[...]
            sin[at, :] = near_sin * row_cos[...] + near_cos * row_sin[...]
            pos = (block * half + lax.broadcasted_iota(jnp.int32, (half, 1), 0)).astype(f32)
            start = jnp.zeros((half, 1), f32)
            for bound in bounds:
                start = jnp.where(pos >= bound, bound, start)
            pos_rows[at, :] = pos
            start_rows[at, :] = start


def column(row):
    n = row.shape[1]
    same = lax.broadcasted_iota(jnp.int32, (n, n), 0) == lax.broadcasted_iota(jnp.int32, (n, n), 1)
    return jnp.sum(jnp.where(same, row, 0.0), axis=1, keepdims=True)


def attention_kernel(plan, x, gain_one, gain_two, pairs, segments, block_cos, block_sin, row_cos, row_sin,
                     dy, w_query, w_key, w_value, wout, w_gate, w_up, wdown,
                     hidden, hhat, ob_local, cos, sin, pos_rows, start_rows, pos_cols,
                     q_out, k_out, v_out, x_all, dy_all, wqkv_all, wout_all, wg_all, wu_own, wdown_all,
                     xhat, wq, wk, wv, wg, wu, x_v, wqkv_v, wout_v, q, k, v, ob, local, loads, *sems):
    place = Place()
    qkv_swap, qkv_seq, out_ring, out_seq, ob_swap, gate_swap, gate_seq, up_swap, down_seq = pairs_of(sems[:18])
    x_grid, dy_grid = sems[18:22], sems[22:26]
    bf16, f32 = jnp.bfloat16, jnp.float32
    rows, width = x.shape
    head, shard = ob.shape[1], wout.shape[0]
    groups = H // KVH
    fetch = [
        pltpu.make_async_copy(src, dst, loads.at[i])
        for i, (src, dst) in enumerate(((w_query, wq), (w_key, wk), (w_value, wv), (w_gate, wg), (w_up, wu)))
    ]
    for copy in fetch:
        copy.start()
    keep = [
        pltpu.make_async_copy(wout, wout_all.at[place.s, place.c], local.at[0]),
        pltpu.make_async_copy(wdown, wdown_all.at[place.s], local.at[1]),
        pltpu.make_async_copy(dy, ByArrival(dy_all, rows, place).owner(place.c), local.at[2]),
    ]
    for copy in keep:
        copy.start()

    def normed(at):
        t = x[at, :].astype(f32)
        xhat[at, :] = (t * lax.rsqrt(jnp.mean(t * t, axis=-1, keepdims=True) + EPSILON)).astype(bf16)

    chunks(rows, 16, normed)
    greet(place.peers() + [place.core_peer, place.far_peer])
    down_w = seq_gather(wdown, wdown_all, down_seq, place)
    x_blocks, dy_blocks = ByOwner(x_all, rows), ByArrival(dy_all, rows, place)

    def out_flow():
        yield from ring_gather(wout, Owners(wout_all.at[place.s], place), out_ring, place)
        keep[0].wait()
        yield from seq_gather(wout_all.at[place.s], wout_all, out_seq, place)

    out_w = out_flow()

    def scale(ref, gain):
        def body(cols):
            ref[:, cols] = (ref[:, cols].astype(f32) * gain).astype(bf16)

        chunks(ref.shape[1], 512, body)

    for copy in fetch[:3]:
        copy.wait()
    gain = column(gain_one[...].astype(f32))
    for ref in (wq, wk, wv):
        scale(ref, gain)

    def spread(pieces, dst, i, swap, seq, group=RING):
        def to(c, into):
            cols = pieces(c)
            each = into.shape[1] // len(cols)
            return [(src, into.at[:, pl.ds(j * each, each)]) for j, src in enumerate(cols)]

        rows_of_s = dst if seq is None else dst.at[place.s]
        own = rows_of_s.at[place.c]
        for src, into in to(place.c, own):
            pltpu.make_async_copy(src, into, local.at[i]).start()
        yield from exchange(lambda o: to(place.at(o), own), lambda o: rows_of_s.at[place.at(o)], swap, place, group)
        pltpu.make_async_copy(own, own, local.at[i]).wait()
        if seq is not None:
            yield from seq_gather(rows_of_s, dst, seq, place)

    def head_columns(t):
        kv = block_at(t // groups, head)
        return [wq.at[:, block_at(t, head)], wk.at[:, kv], wv.at[:, kv]]

    def unit_columns(ref):
        own = wdown.shape[0]
        return lambda t: [ref.at[:, block_at(i * RING + t, own)] for i in range(SEQ)]

    qkv_w = spread(head_columns, wqkv_all, 3, qkv_swap, qkv_seq)
    gate_w = spread(unit_columns(wg), wg_all, 4, gate_swap, gate_seq, 2)
    up_w = spread(unit_columns(wu), wu_own, 5, up_swap, None, 2)
    x_flow = grid_gather(xhat, x_blocks, x_grid, place)
    dy_flow = grid_gather(dy, dy_blocks, dy_grid, place)
    own_x = pltpu.make_async_copy(xhat, x_blocks.owner(place.c), local.at[6])

    flows = {"q": qkv_w, "g": gate_w, "u": up_w, "d": down_w, "o": out_w, "x": x_flow, "y": dy_flow}
    mine = block_at(place.c, head)
    flows["b"] = exchange(
        lambda o: [(ob.at[block_at(place.at(o), rows)], ob_local.at[:, mine])],
        lambda o: ob_local.at[:, block_at(place.at(o), head)],
        ob_swap,
        place,
    )
    load = [pltpu.make_async_copy(x_all, x_v, loads.at[0]), pltpu.make_async_copy(wqkv_all, wqkv_v, loads.at[1])]
    saves = [pltpu.make_async_copy(src, dst, loads.at[2 + i]) for i, (src, dst) in enumerate(((q, q_out), (k, k_out), (v, v_out)))]
    load_out = pltpu.make_async_copy(wout_all, wout_v, local.at[0])

    def scale_units():
        for copy in fetch[3:]:
            copy.wait()
        gain = column(gain_two[...].astype(f32))
        scale(wg, gain)
        scale(wu, gain)

    def find_rows():
        place_rows(
            pairs, segments, block_cos, block_sin, row_cos, row_sin, cos, sin, pos_rows, start_rows, pos_cols
        )

    def load_attention():
        own_x.start()
        own_x.wait()
        for copy in load:
            copy.start()

    def project_all():
        for copy in load:
            copy.wait()

        def project(at):
            qkv = dot(x_v[at, :], wqkv_v[...].reshape(width, 3 * head))
            c, s = cos[at, :], sin[at, :]
            q[at, :] = turned(qkv[:, :head], c, s, 1.0).astype(bf16)
            k[at, :] = turned(qkv[:, head : 2 * head], c, s, 1.0).astype(bf16)
            v[at, :] = qkv[:, 2 * head :].astype(bf16)

        chunks(x_v.shape[0], 256, project)
        for copy in saves:
            copy.start()

    def attend_all():
        def attend(at):
            prob = probabilities(q[at, :], k[...], pos_rows[at, :], start_rows[at, :], pos_cols[...])
            ob[at, :] = dot(prob.astype(bf16), v[...]).astype(bf16)

        chunks(x_v.shape[0], 256, attend)
        ob_local[:, mine] = ob[block_at(place.c, rows), :]

    def finish_hidden():
        load_out.wait()

        def residual(cols):
            part = dot(ob_local[...], wout_v[:, :, :, cols].reshape(width, cols.size))
            hidden[:, cols] = x[:, cols].astype(f32) + part

        chunks(width, 256, residual)

        def normed_two(at):
            t = hidden[at, :]
            hhat[at, :] = (t * lax.rsqrt(jnp.mean(t * t, axis=-1, keepdims=True) + EPSILON)).astype(bf16)

        chunks(rows, 16, normed_two)

    works = {
        "S": scale_units, "R": find_rows, "L": load_attention, "P": project_all,
        "A": attend_all, "W": load_out.start, "H": finish_hidden,
    }
    for step in plan:
        if step in flows:
            next(flows[step], None)
        else:
            works[step]()
    for name, flow in flows.items():
        if name in plan:
            for _ in flow:
                pass
    if "P" in plan:
        for copy in saves:
            copy.wait()
    elif "L" in plan:
        for copy in load:
            copy.wait()
    if "S" not in plan:
        for copy in fetch[3:]:
            copy.wait()
    if "o" not in plan:
        keep[0].wait()
    if "W" in plan and "H" not in plan:
        load_out.wait()
    keep[1].wait()
    keep[2].wait()


def mlp_kernel(plan, hhat, dy_hbm, wg_hbm, wu_own, wdown_hbm, sum_h, sum_o, col_out, down_out,
               h_all, dy_all, wg, wu, wd, mid, dgate, dup, stage_h, stage_o, stage, stage_2, slots_h, slots_o,
               col_sent, col_near, col_far, down_sent, down_near, down_far, local, *sems):
    place = Place()
    h_sems, sum_h_sems, sum_o_sems, col_seq, down_seq, up_seq = pairs_of(sems)
    greet([place.right, place.left, place.core_peer, place.far_peer])
    rows, width = hhat.shape
    ff = wg.shape[1]
    bf16, f32 = jnp.bfloat16, jnp.float32
    up_blocks = Blocks(wu, wu_own.shape[0])
    keep = [
        pltpu.make_async_copy(src, dst, local.at[i])
        for i, (src, dst) in enumerate(
            ((hhat, h_all.at[pl.ds(0, rows)]), (wg_hbm, wg), (wu_own, up_blocks[place.s]), (wdown_hbm, wd), (dy_hbm, dy_all))
        )
    ]
    for copy in keep:
        copy.start()
    gather = ring_gather(hhat, Rows(h_all, rows), h_sems, place)
    up_flow = seq_gather(wu_own, up_blocks, up_seq, place)

    def hidden_rows(start, count):
        at = pl.ds(start, count)

        def body(cols):
            gate = dot(h_all[at, :], wg[:, cols])
            up = dot(h_all[at, :], wu[:, cols])
            dmid = dot(dy_all[at, :], wd[cols, :], (1, 1))
            sig = jax.nn.sigmoid(gate)
            active = gate * sig
            mid[at, cols] = (active * up).astype(bf16)
            dgate[at, cols] = (dmid * up * sig * (1.0 + gate * (1.0 - sig))).astype(bf16)
            dup[at, cols] = (dmid * active).astype(bf16)

        chunks(ff, 512, body)

    def part_h(start, count, dst):
        at = pl.ds(start, count)

        def body(cols):
            dst[:, cols] = (dot(dgate[at, :], wg[cols, :], (1, 1)) + dot(dup[at, :], wu[cols, :], (1, 1))).astype(bf16)

        chunks(width, 512, body)

    def part_o(start, count, dst):
        at = pl.ds(start, count)

        def body(cols):
            dst[:, cols] = dot(mid[at, :], wd[:, cols]).astype(bf16)

        chunks(width, 1024, body)

    def col_grad(s, dst, add):
        def body(cols):
            lhs = h_all[:, pl.ds(pl.multiple_of(s * dst.shape[0] + cols.start, 256), 256)]
            for side, grad in enumerate((dgate, dup)):
                there = pl.ds(side * ff, ff)
                value = dot(lhs, grad[...], (0, 0))
                if add:
                    value = value + dst[cols, there].astype(f32)
                dst[cols, there] = value.astype(bf16)

        chunks(dst.shape[0], 256, body)

    def down_grad(s, dst, add):
        lhs = pl.ds(pl.multiple_of(s * dst.shape[0], 256), dst.shape[0])

        def body(cols):
            value = dot(mid[:, lhs], dy_all[:, cols], (0, 0))
            if add:
                value = value + dst[:, cols].astype(f32)
            dst[:, cols] = value.astype(bf16)

        chunks(width, 1024, body)

    def pair(ref):
        return (ref.at[pl.ds(rows, rows)], ref.at[pl.ds(0, rows)])

    col_sum = SeqSum(col_grad, col_sent, col_near, col_far, col_seq, place)
    down_sum = SeqSum(down_grad, down_sent, down_near, down_far, down_seq, place)
    ring_h, ring_o = RingSum(slots_h, sum_h_sems, place), RingSum(slots_o, sum_o_sems, place)
    top_h, top_o = stage_h.at[pl.ds(2 * rows, rows)], stage_o.at[pl.ds(2 * rows, rows)]
    next_h, next_o = stage_h.at[pl.ds(0, 2 * rows)], stage_o.at[pl.ds(0, 2 * rows)]

    def in_turn(*actions):
        return iter(actions)

    def parts(part, top, following, later):
        return in_turn(
            lambda: part(7 * rows, rows, top),
            lambda: part(5 * rows, 2 * rows, following),
            lambda: part(3 * rows, 2 * rows, later),
            lambda: part(rows, 2 * rows, later),
            lambda: part(0, rows, later.at[pl.ds(0, rows)]),
        )

    def sums(ring, top, following, later, out):
        return in_turn(
            lambda: ring.first(top),
            lambda: ring.relay(1, pair(following)),
            lambda: ring.relay(2, pair(later)),
            lambda: ring.relay(3, pair(later)),
            lambda: ring.last(later.at[pl.ds(0, rows)], out),
        )

    def wait_loads():
        for copy in keep:
            copy.wait()

    turns = {
        "k": in_turn(wait_loads),
        "a": in_turn(lambda: hidden_rows(0, rows)),
        "b": in_turn(lambda: hidden_rows(rows, 2 * rows)),
        "c": in_turn(lambda: hidden_rows(3 * rows, 2 * rows)),
        "d": in_turn(lambda: hidden_rows(5 * rows, 2 * rows)),
        "e": in_turn(lambda: hidden_rows(7 * rows, rows)),
        "P": parts(part_h, top_h, next_h, stage),
        "r": sums(ring_h, top_h, next_h, stage, sum_h),
        "O": parts(part_o, top_o, next_o, stage_2),
        "s": sums(ring_o, top_o, next_o, stage_2, sum_o),
        "n": in_turn(lambda: col_sum.near(0), lambda: col_sum.near(1)),
        "m": in_turn(col_sum.across),
        "w": in_turn(col_sum.own),
        "l": in_turn(col_sum.last),
        "N": in_turn(lambda: down_sum.near(0), lambda: down_sum.near(1)),
        "M": in_turn(down_sum.across),
        "W": in_turn(down_sum.own),
        "L": in_turn(down_sum.last),
    }
    for step in plan:
        if step == "x":
            next(gather)
        elif step == "u":
            next(up_flow)
        else:
            next(turns[step])()
    ends = []
    for i, (total, out) in enumerate(((col_sum, col_out), (down_sum, down_out))):
        ends.append(pltpu.make_async_copy(total.far, out, local.at[i]))
        ends[-1].start()
    for copy in ends:
        copy.wait()
    for flow in (ring_h, ring_o, col_sum, down_sum):
        flow.end()
    for flow in (gather, up_flow):
        for _ in flow:
            pass


def backward_kernel(plan, weighted, hidden, dy, x, q, k, v, ob_local, cos, sin, pos_rows, start_rows, pos_cols,
                    x_all, wqkv_all, wout_all, col,
                    grad_x, out_grad, qkv_raw, gate_raw, up_raw, col_in,
                    x_v, wqkv_v, wout_v, branch, datt_own, datt, dqkv, dk, dv, sum_x, over_x, line_x,
                    qkv_sent, qkv_near, qkv_far, qkv_in, out_sent, out_near, out_far, slots_o, local, *sems):
    place = Place()
    att_swap, col_swap, qkv_seq, qkv_swap, out_seq, out_ring = pairs_of(sems[:12])
    x_grid = sems[12:]
    bf16, f32 = jnp.bfloat16, jnp.float32
    rows, width = x.shape
    head = q.shape[1]
    seq_len = q.shape[0]
    shard = out_grad.shape[0]
    loads = [
        pltpu.make_async_copy(src, dst, local.at[i])
        for i, (src, dst) in enumerate(((wout_all, wout_v), (x_all, x_v), (wqkv_all, wqkv_v)))
    ]
    for copy in loads:
        copy.start()
    col_blocks, qkv_blocks = Blocks(col, shard), Blocks(qkv_far, shard)
    own_col = pltpu.make_async_copy(col_blocks[place.c], col_in.at[place.c], local.at[3])
    own_col.start()
    greet(place.peers() + [place.core_peer, place.far_peer])
    def norm_back(tensor, grads):
        scale = lax.rsqrt(jnp.mean(tensor * tensor, axis=-1, keepdims=True) + EPSILON)
        inner = jnp.mean(grads * tensor, axis=-1, keepdims=True)
        return scale * grads - tensor * (scale * scale * scale) * inner

    def hidden_back(at):
        grads = dy[at, :].astype(f32) + norm_back(hidden[at, :], weighted[at, :])
        grad_x[at, :] = grads
        branch[at, :] = grads.astype(bf16)

    def heads_back():
        chunks(rows, 16, hidden_back)
        loads[0].wait()

        def att_back(cols):
            datt_own[:, cols] = dot(branch[...], wout_v[cols, :], (1, 1)).astype(bf16)

        chunks(width, head, att_back)

    mine = block_at(place.c, rows)
    att_flow = exchange(
        lambda o: [(datt_own.at[:, block_at(place.at(o), head)], datt.at[mine])],
        lambda o: datt.at[block_at(place.at(o), rows)],
        att_swap,
        place,
    )
    def rows_grad(left, right):
        def grad(s, dst, add):
            def body(cols):
                lhs = left[:, pl.ds(pl.multiple_of(s * dst.shape[0] + cols.start, 256), 256)]
                value = dot(lhs, right[...], (0, 0))
                if add:
                    value = value + dst[cols, :].astype(f32)
                dst[cols, :] = value.astype(bf16)

            chunks(dst.shape[0], 256, body)

        return grad

    out_sum = SeqSum(rows_grad(ob_local, branch), out_sent, out_near, out_far, out_seq, place)
    qkv_sum = SeqSum(rows_grad(x_v, dqkv), qkv_sent, qkv_near, qkv_far, qkv_seq, place)
    def attend_back(at):
        prob = probabilities(q[at, :], k[...], pos_rows[at, :], start_rows[at, :], pos_cols[...])
        dprob = dot(datt[at, :], v[...], (1, 1))
        delta = jnp.sum(prob * dprob, axis=-1, keepdims=True)
        dscore = (prob * (dprob - delta)).astype(bf16)
        dq = dot(dscore, k[...]) * HDIM ** (-0.5)
        dqkv[at, pl.ds(0, head)] = turned(dq, cos[at, :], sin[at, :], -1.0).astype(bf16)
        dk[...] += dot(dscore, q[at, :], (0, 0))
        dv[...] += dot(prob.astype(bf16), datt[at, :], (0, 0))

    def finish_back(at):
        turned_dk = turned(dk[at, :] * HDIM ** (-0.5), cos[at, :], sin[at, :], -1.0)
        dqkv[at, pl.ds(head, head)] = turned_dk.astype(bf16)
        dqkv[at, pl.ds(2 * head, head)] = dv[at, :].astype(bf16)

    def all_back():
        dk[...] = jnp.zeros_like(dk)
        dv[...] = jnp.zeros_like(dv)
        datt[mine, :] = datt_own[:, block_at(place.c, head)]
        for copy in loads[1:]:
            copy.wait()
        chunks(seq_len, 256, attend_back)
        chunks(seq_len, 128, finish_back)

    part = wout_v.at[pl.ds(0, seq_len)]
    total = GridSum(part, over_x, line_x, x_grid, place)

    def part_x(i):
        at = block_at(total.plane(i), 2 * rows)

        def body(cols):
            part[at, cols] = dot(dqkv[at, :], wqkv_v[cols, :], (1, 1)).astype(bf16)

        chunks(width, 1024, body)
        total.across(i)

    unit = gate_raw.shape[1] // (RING * SEQ)
    groups = H // KVH

    def move_columns():
        own_col.wait()
        for c in range(RING):
            for side, raw in enumerate((gate_raw, up_raw)):
                for i in range(SEQ):
                    src = col_in.at[c, :, pl.ds((side * SEQ + i) * unit, unit)]
                    into = raw.at[:, pl.ds((i * RING + c) * unit, unit)]
                    pltpu.make_async_copy(src, into, local.at[4 + side]).start()

    own_qkv = pltpu.make_async_copy(qkv_blocks[place.c], qkv_in.at[place.c], local.at[6])

    def qkv_last():
        qkv_sum.last()
        own_qkv.start()

    def tokens_back():
        total.last(sum_x)

        def token_back(at):
            grad_x[at, :] = grad_x[at, :] + norm_back(x[at, :].astype(f32), sum_x[at, :])

        chunks(rows, 16, token_back)

    def finish_qkv():
        own_qkv.wait()
        for t in range(H):
            qkv_raw[:, pl.ds(t * head, head)] = qkv_in[t, :, pl.ds(0, head)].astype(f32)
        for side in (1, 2):
            for t in range(KVH):
                value = sum(qkv_in[t * groups + g, :, pl.ds(side * head, head)].astype(f32) for g in range(groups))
                qkv_raw[:, pl.ds((H + (side - 1) * KVH + t) * head, head)] = value

    def each(action, count=4):
        return iter([functools.partial(action, i) for i in range(count)])

    out_blocks = Owners(Blocks(out_far, shard), place)
    flows = {
        "a": att_flow,
        "c": by_owner(col_blocks, col_in, col_swap, place, 2),
        "o": ring_scatter(out_blocks, out_grad, slots_o, out_ring, place),
        "t": by_owner(qkv_blocks, qkv_in, qkv_swap, place),
    }
    works = {
        "h": heads_back, "B": all_back, "m": out_sum.across, "w": out_sum.own, "e": out_sum.last,
        "M": qkv_sum.across, "W": qkv_sum.own, "E": qkv_last, "V": move_columns, "Z": tokens_back, "F": finish_qkv,
    }
    turns = {"n": each(out_sum.near, 2), "N": each(qkv_sum.near, 2), "p": each(part_x), "l": each(total.along, 3)}
    for step in plan:
        if step in flows:
            next(flows[step])
        elif step in turns:
            next(turns[step])()
        else:
            works[step]()
    if "V" in plan:
        for raw, sem in ((gate_raw, local.at[4]), (up_raw, local.at[5])):
            pltpu.make_async_copy(raw, raw, sem).wait()
    else:
        own_col.wait()
    for name, flow in flows.items():
        if name in plan:
            for _ in flow:
                pass
    for flow in (total, out_sum, qkv_sum):
        flow.end()


class Blocks:
    def __init__(self, ref, rows):
        self.ref, self.rows = ref, rows
        self.shape = (ref.shape[0] // rows, rows) + tuple(ref.shape[1:])

    @property
    def at(self):
        return self

    def __getitem__(self, i):
        return self.ref.at[pl.ds(pl.multiple_of(i * self.rows, self.rows), self.rows)]


DMA = pltpu.SemaphoreType.DMA
HBM = pl.ANY


ATTENTION_PLAN = "dqxoooxoooxooRqqoooxxSggggqqLyPAbygggyuuuuyooWyybHdgu"


def attention_stage(
    tokens, cotangent, gain_attn, w_query, w_key, w_value, w_out, gain_mlp, w_gate, w_up, w_down, pair_order, segments, plan
):
    bf16, f32 = jnp.bfloat16, jnp.float32
    n = RING
    rows, width = tokens.shape[1], tokens.shape[2]
    seq_len = segments.shape[1]
    shard = w_query.shape[0]
    ff_own = w_down.shape[0]
    ff_mine = SEQ * ff_own
    head = HDIM
    frequency = THETA ** (-(np.arange(head // 2) * 2.0 / head))
    half = rows // 2
    block_angles = np.arange(2 * n)[:, None] * half * frequency[None, :]
    row_angles = np.arange(half)[:, None] * frequency[None, :]
    tables = tuple(jnp.asarray(f(angles), f32) for angles in (block_angles, row_angles) for f in (np.cos, np.sin))

    return call(
        functools.partial(attention_kernel, plan),
        [
            shaped((rows, width), f32),
            shaped((rows, width)),
            shaped((rows, H * head)),
            shaped((seq_len, head // 2), f32),
            shaped((seq_len, head // 2), f32),
            shaped((seq_len, 1), f32),
            shaped((seq_len, 1), f32),
            shaped((1, seq_len), f32),
            shaped((seq_len, head)),
            shaped((seq_len, head)),
            shaped((seq_len, head)),
            shaped((seq_len, width)),
            shaped((seq_len, width)),
            shaped((SEQ, n, shard, 3 * head)),
            shaped((SEQ, n, shard, width)),
            shaped((SEQ, n, shard, ff_mine)),
            shaped((n, shard, ff_mine)),
            shaped((SEQ, ff_own, width)),
        ],
        (tokens[0], gain_attn[None], gain_mlp[None], pair_order, segments)
        + tables
        + (cotangent[0], w_query, w_key, w_value, w_out, w_gate, w_up, w_down),
        [VMEM] * 3 + [pltpu.SMEM] + [VMEM] * 5 + [HBM] * 8,
        [VMEM] * 8 + [HBM] * 10,
        [
            VMEM((rows, width), bf16),
            VMEM(w_query.shape, bf16),
            VMEM(w_key.shape, bf16),
            VMEM(w_value.shape, bf16),
            VMEM(w_gate.shape, bf16),
            VMEM(w_up.shape, bf16),
            VMEM((seq_len, width), bf16),
            VMEM((SEQ, n, shard, 3 * head), bf16),
            VMEM((SEQ, n, shard, width), bf16),
        ]
        + [VMEM((seq_len, head), bf16)] * 4
        + [DMA((7,)), DMA((5,))]
        + pair_sems()
        + seq_sems()
        + ring_sems()
        + seq_sems()
        + pair_sems()
        + (pair_sems() + seq_sems()) * 2
        + grid_sems() * 2,
        1,
    )


MLP_PLAN = "xuxkxxuxxuabxxxcdxePrnPrnmOsPrOsNPrNMOsPwrOsOWslL"


def mlp_stage(hhat, dy_all, wg_all, wu_own, wdown_all, plan):
    bf16, f32, n = jnp.bfloat16, jnp.float32, RING
    (rows, width), seq_len = hhat.shape, dy_all.shape[0]
    ff_mine = wg_all.shape[1]
    shard, ff_own = width // (SEQ * n), ff_mine // SEQ
    slot_shape = VMEM((2, n // 2, rows, width), bf16)
    col_piece, down_piece = (n * shard, 2 * ff_mine), (ff_own, width)
    return call(
        functools.partial(mlp_kernel, plan),
        [shaped((rows, width), f32)] * 2 + [shaped(col_piece), shaped(down_piece)],
        (hhat, dy_all, wg_all, wu_own, wdown_all),
        [HBM] * 5,
        [VMEM] * 2 + [HBM] * 2,
        [VMEM((seq_len, width), bf16)] * 2
        + [VMEM((width, ff_mine), bf16)] * 2
        + [VMEM((ff_mine, width), bf16)]
        + [VMEM((seq_len, ff_mine), bf16)] * 3
        + [VMEM((3 * rows, width), bf16)] * 2
        + [VMEM((2 * rows, width), bf16)] * 2
        + [slot_shape] * 2
        + [VMEM((2,) + col_piece, bf16), VMEM((2,) + col_piece, bf16), VMEM(col_piece, bf16)]
        + [VMEM((2,) + down_piece, bf16), VMEM((2,) + down_piece, bf16), VMEM(down_piece, bf16)]
        + [DMA((5,))]
        + ring_sems() * 3
        + seq_sems() * 3,
        2,
    )


BACKWARD_PLAN = "channmacccBppNpNplMlwWclEtVZteooooFo"


def backward_stage(args, columns, plan):
    bf16, f32, n, head = jnp.bfloat16, jnp.float32, RING, HDIM
    (rows, width), seq_len, shard = args[0].shape, args[4].shape[0], columns[0]
    ff_mine = columns[1] // n
    piece = (n * shard, width)
    qkv_piece = (n * shard, 3 * head)
    outs = call(
        functools.partial(backward_kernel, plan),
        [
            shaped((rows, width), f32),
            shaped((shard, width), f32),
            shaped((shard, (H + 2 * KVH) * head), f32),
            shaped(columns),
            shaped(columns),
            shaped((n, shard, 2 * ff_mine)),
        ],
        args,
        [VMEM] * 13 + [HBM] * 4,
        [VMEM] * 3 + [HBM] * 3,
        [
            VMEM((seq_len, width), bf16),
            VMEM((width, 3 * head), bf16),
            VMEM((H * head, width), bf16),
            VMEM((rows, width), bf16),
            VMEM((rows, width), bf16),
            VMEM((seq_len, head), bf16),
            VMEM((seq_len, 3 * head), bf16),
            VMEM((seq_len, head), f32),
            VMEM((seq_len, head), f32),
            VMEM((rows, width), f32),
            VMEM((n // 2, rows, width), bf16),
            VMEM((2, n // 2, rows, width), bf16),
        ]
        + [VMEM((2,) + qkv_piece, bf16), VMEM((2,) + qkv_piece, bf16), VMEM(qkv_piece, bf16)]
        + [VMEM((n, shard, 3 * head), bf16)]
        + [VMEM((2,) + piece, bf16), VMEM((2,) + piece, bf16), VMEM(piece, bf16)]
        + [VMEM((2, n // 2, shard, width), bf16), DMA((7,))]
        + pair_sems() * 2
        + seq_sems()
        + pair_sems()
        + seq_sems()
        + ring_sems()
        + grid_sum_sems(),
        5,
    )
    return outs[:-1]


def ring_device(
    tokens, cotangent, gain_attn, w_query, w_key, w_value, w_out, gain_mlp, w_gate, w_up, w_down, pair_order, segments
):
    bf16, f32 = jnp.bfloat16, jnp.float32
    n = RING
    rows, width = tokens.shape[1], tokens.shape[2]
    seq_len = segments.shape[1]
    shard = w_query.shape[0]
    ff_own = w_down.shape[0]
    ff_mine = SEQ * ff_own
    head = HDIM
    outs = attention_stage(
        tokens, cotangent, gain_attn, w_query, w_key, w_value, w_out, gain_mlp, w_gate, w_up, w_down,
        pair_order, segments, ATTENTION_PLAN,
    )
    hidden, hhat, ob_local = outs[:3]
    where = outs[3:8]
    q, k, v, x_all, dy_all, wqkv_all, wout_all, wg_all, wu_own, wdown_all = outs[8:]
    wqkv_all = wqkv_all.reshape(width, 3 * head)
    wout_all = wout_all.reshape(H * head, width)
    wg_all = wg_all.reshape(width, ff_mine)
    wu_own = wu_own.reshape(n * shard, ff_mine)
    wdown_all = wdown_all.reshape(ff_mine, width)
    dweighted, out_sum, col_sum, down_sum = mlp_stage(hhat, dy_all, wg_all, wu_own, wdown_all, MLP_PLAN)
    output = (hidden + out_sum).astype(bf16)[None]

    grad_tokens, out_grad, qkv_raw, gate_raw, up_raw = backward_stage(
        (dweighted, hidden, cotangent[0], tokens[0], q, k, v, ob_local)
        + tuple(where)
        + (x_all, wqkv_all, wout_all, col_sum),
        w_gate.shape, BACKWARD_PLAN,
    )
    gain_one = gain_attn.astype(f32)[:, None]
    gain_two = gain_mlp.astype(f32)[:, None]
    raw_q = qkv_raw[:, : H * head]
    raw_k = qkv_raw[:, H * head : (H + KVH) * head]
    raw_v = qkv_raw[:, (H + KVH) * head :]

    def gain_part(raw, w):
        return jnp.sum(raw.astype(f32) * w.astype(f32), axis=1)

    grad_gain_one = gain_part(raw_q, w_query) + gain_part(raw_k, w_key) + gain_part(raw_v, w_value)
    grad_gain_two = gain_part(gate_raw, w_gate) + gain_part(up_raw, w_up)
    return (
        output,
        grad_tokens[None],
        grad_gain_one,
        raw_q * gain_one,
        raw_k * gain_one,
        raw_v * gain_one,
        out_grad,
        grad_gain_two,
        gate_raw.astype(f32) * gain_two,
        up_raw.astype(f32) * gain_two,
        down_sum.astype(f32),
    )


def solution(mesh):
    placed = (
        P("seq", "ctx", None),
        P("seq", "ctx", None),
        P(("seq", "ctx")),
        P(("seq", "ctx"), None),
        P(("seq", "ctx"), None),
        P(("seq", "ctx"), None),
        P(("seq", "ctx"), None),
        P(("seq", "ctx")),
        P(("seq", "ctx"), None),
        P(("seq", "ctx"), None),
        P(("seq", "ctx"), None),
        P("seq", None),
        P("seq", None),
    )
    fits = mesh.shape["ctx"] == H and mesh.shape["seq"] == 4
    chosen = ring_device if fits else general_device
    return jax.shard_map(
        chosen,
        mesh=mesh,
        in_specs=placed,
        out_specs=(
            P("seq", "ctx", None),
            P("seq", "ctx", None),
            P(("seq", "ctx")),
            P(("seq", "ctx"), None),
            P(("seq", "ctx"), None),
            P(("seq", "ctx"), None),
            P(("seq", "ctx"), None),
            P(("seq", "ctx")),
            P(("seq", "ctx"), None),
            P(("seq", "ctx"), None),
            P(("seq", "ctx"), None),
        ),
        check_vma=False,
    )
```

profile of v0, /device:TPU:0, one launch (start us, length us, event | category | flops | bytes accessed | tf_op | source)
XLA Modules:
  0.0 491.8 jit_solution(7751332829691811591)
XLA Ops:
  0.6 192.1 %shard_map.248 = (f32[128,2048]{1,0:T(8,128)}, bf16[128,2048]{1,0:T(8,128)(2,1)}, bf16[128,2048]{1,0:T(8,128)(2,1)}, f32[1024,128]{1,0:T(8,128)}, f32[1024,128]{...) custom-call(bf16[128,2048]{1,0:T(8,128)(2,1)} %bitcast.16, ...), custom_call_target="tpu_custom_call" | custom-call | tf_op jit(solution)/shard_map/pallas_call | solution.py:790
  192.8 140.1 %shard_map.249 = (f32[128,2048]{1,0:T(8,128)}, f32[128,2048]{1,0:T(8,128)}, bf16[512,2048]{1,0:T(8,128)(2,1)}, bf16[256,2048]{1,0:T(8,128)(2,1)}) custom-call(bf16[128,2048]{1,0:T(8,128)(2,1)} %get-tuple-element.39.hhat, bf16[1024,2048]{1,0:T(8,128)(2,1)} %get-tuple-element.40.dy_hbm, bf16[2048,1024]{1,0:T(8,128)(2,1)} %bitcast.13, ...), custom_call_target="tpu_custom_call" | custom-call | tf_op jit(solution)/shard_map/pallas_call | solution.py:790
  332.9 0.0 copy-start.9
  332.9 145.8 %shard_map.250 = (f32[128,2048]{1,0:T(8,128)}, f32[64,2048]{1,0:T(8,128)}, f32[64,4096]{1,0:T(8,128)}, bf16[64,8192]{1,0:T(8,128)(2,1)}, bf16[64,8192]{1,0:T(8,128)(2,1)}, /*index=5*/bf16[8,64,2048]{2,1,0:T(8,128)(2,1)}) custom-call(f32[128,2048]{1,0:T(8,128)} %get-tuple-element.45.weighted, f32[128,2048]{1,0:T(8,128)} %get-tuple-element.38.hidden, ...), custom_call_target="tpu_custom_call" | custom-call | tf_op jit(solution)/shard_map/pallas_call | solution.py:790
  478.7 0.0 copy-done.9
  478.7 0.0 copy-start.10
  478.7 0.0 copy-start.4
  478.7 0.0 copy-start.7
  478.7 0.0 copy-start.8
  478.8 0.0 copy-start.5
  478.8 5.1 %convert_multiply_fusion = (f32[64,8192]{1,0:T(8,128)}, f32[64]{0:T(128)S(1)}, f32[64]{0:T(128)S(1)}, f32[64,8192]{1,0:T(8,128)}) fusion(bf16[64,8192]{1,0:T(8,128)(2,1)} %get-tuple-element.63, f32[64]{0:T(128)S(1)} %convert_element_type.44, bf16[64,8192]{1,0:T(8,128)(2,1)} %w_up.1, bf16[64,8192]{1,0:T(8,128)(2,1)} %w_gate.1, bf16[64,8192]{1,0:T(8,128)(2,1)} %get-tuple-element.62), kind=kLoop, calls=%fused_computation | loop fusion | flops 5242752 | bytes 8389376 | tf_op jit(solution)/shard_map/mul | solution.py:1587
  483.9 0.0 copy-start.1
  483.9 0.5 add.15
  484.4 0.0 copy-done.10
  484.4 0.0 copy-done.4
  484.4 0.0 copy-done.7
  484.4 0.0 copy-done.8
  484.5 1.0 slice_multiply_fusion.1
  485.5 0.0 copy-done.5
  485.5 0.0 copy-start
  485.5 0.0 copy-start.2
  485.5 1.0 slice_multiply_fusion
  486.5 0.5 add_add_fusion
  487.0 0.0 copy-done.1
  487.0 1.6 convert_element_type.45
  488.6 0.0 copy-start.3
  488.6 0.0 copy-done
  488.6 0.0 copy-done.2
  488.6 0.0 copy-start.6
  488.6 0.9 fusion.2
  489.5 0.5 copy-done.3
  490.0 1.0 copy.30
  491.0 0.0 copy-done.6
  491.0 0.8 copy.31
  (2 shorter events, 0.0 us)
Async XLA Ops:
  332.9 145.8 %copy-start.9 = (bf16[64]{0:T(256)(128)(2,1)S(1)}, bf16[64]{0:T(256)(128)(2,1)}, u32[]{:S(2)}) copy-start(bf16[64]{0:T(256)(128)(2,1)} %param.24) | copy-start | bytes 388
  478.7 5.7 %copy-start.10 = (bf16[64]{0:T(256)(128)(2,1)S(1)}, bf16[64]{0:T(256)(128)(2,1)}, u32[]{:S(2)}) copy-start(bf16[64]{0:T(256)(128)(2,1)} %param.19) | copy-start | bytes 388
  478.7 5.7 %copy-start.4 = (f32[64,4096]{1,0:T(8,128)S(1)}, f32[64,4096]{1,0:T(8,128)}, u32[]{:S(2)}) copy-start(f32[64,4096]{1,0:T(8,128)} %get-tuple-element.60) | copy-start | bytes 3145732
  478.7 5.7 %copy-start.7 = (bf16[64,1024]{1,0:T(8,128)(2,1)S(1)}, bf16[64,1024]{1,0:T(8,128)(2,1)}, u32[]{:S(2)}) copy-start(bf16[64,1024]{1,0:T(8,128)(2,1)} %w_key.1) | copy-start | bytes 393220
  478.7 5.7 %copy-start.8 = (bf16[64,1024]{1,0:T(8,128)(2,1)S(1)}, bf16[64,1024]{1,0:T(8,128)(2,1)}, u32[]{:S(2)}) copy-start(bf16[64,1024]{1,0:T(8,128)(2,1)} %w_value.1) | copy-start | bytes 393220
  478.8 6.7 %copy-start.5 = (bf16[64,2048]{1,0:T(8,128)(2,1)S(1)}, bf16[64,2048]{1,0:T(8,128)(2,1)}, u32[]{:S(2)}) copy-start(bf16[64,2048]{1,0:T(8,128)(2,1)} %w_query.1) | copy-start | bytes 786436
  483.9 3.1 copy-start.1
  485.5 3.1 copy-start
  485.5 3.1 copy-start.2
  488.6 1.4 copy-start.3
  488.6 2.4 copy-start.6
where the time goes:
time: 495 us; the launch traced here: 492 us
  Pallas kernels  478 us (97%)
  other arithmetic  10.6 us (2%)
    pallas_call x3, Pallas kernels, call(): pl.pallas_call(body, out_shape=outs, in_specs=[pl.BlockSpec(memory_space=...  478 us

commit v1 on v0

--- a/solution.py
+++ b/solution.py
@@ -387,10 +387,12 @@
         return [{"ctx": lax.rem(self.c + k, RING)} for k in range(1, RING)]
 
 
-def greet(devices):
+def greet(devices, work=None):
     barrier = pltpu.get_barrier_semaphore()
     for device in devices:
         pl.semaphore_signal(barrier, inc=1, device_id=device, device_id_type=MESH)
+    if work is not None:
+        work()
     pl.semaphore_wait(barrier, len(devices))
 
 
@@ -593,7 +595,7 @@
     return [pltpu.SemaphoreType.DMA((2, 3))] * 2 + [pltpu.SemaphoreType.DMA((4,))] * 2
 
 
-def grid_gather(own, blocks, sems, place):
+def grid_gather(own, blocks, sems, place, late=False):
     z_sems, x_sems = sems[:2], sems[2:]
     z, x = place.z, place.x
     sent = []
@@ -608,7 +610,8 @@
 
     send(z < 3, own, place.c, "up", z_sems, (0, 0), place.up)
     send(z > 0, own, place.c, "down", z_sems, (1, 0), place.down)
-    across(z >= 0, own, z)
+    if not late:
+        across(z >= 0, own, z)
     yield
     for hop in range(1, 4):
         for d, (line, here, further) in enumerate(((z - hop, z >= hop, z < 3), (z + hop, z <= 3 - hop, z > 0))):
@@ -622,8 +625,15 @@
 
             if hop < 3:
                 send(here & further, ref, jnp.clip(index, 0, RING - 1), ("up", "down")[d], z_sems, (d, hop), (place.up, place.down)[d])
-            across_line = jnp.clip(line, 0, 3)
-            send(here, ref, 2 * across_line + x, "side", x_sems, across_line, place.side)
+            if not late:
+                across_line = jnp.clip(line, 0, 3)
+                send(here, ref, 2 * across_line + x, "side", x_sems, across_line, place.side)
+        yield
+    if late:
+        across(z >= 0, own, z)
+        for hop in range(1, 4):
+            line = lax.rem(z + hop, 4)
+            across(z >= 0, blocks.owner(2 * line + x), line)
         yield
     for line in range(4):
         arrived(blocks.owner(2 * line + 1 - x), x_sems, line, place.side)
@@ -863,7 +873,7 @@
                      dy, w_query, w_key, w_value, wout, w_gate, w_up, wdown,
                      hidden, hhat, ob_local, cos, sin, pos_rows, start_rows, pos_cols,
                      q_out, k_out, v_out, x_all, dy_all, wqkv_all, wout_all, wg_all, wu_own, wdown_all,
-                     xhat, wq, wk, wv, wg, wu, x_v, wqkv_v, wout_v, q, k, v, ob, local, loads, *sems):
+                     xhat, wq, wk, wv, wg, wu, heads, gate_units, up_units, x_v, wqkv_v, wout_v, q, k, v, ob, local, loads, *sems):
     place = Place()
     qkv_swap, qkv_seq, out_ring, out_seq, ob_swap, gate_swap, gate_seq, up_swap, down_seq = pairs_of(sems[:18])
     x_grid, dy_grid = sems[18:22], sems[22:26]
@@ -889,8 +899,23 @@
         t = x[at, :].astype(f32)
         xhat[at, :] = (t * lax.rsqrt(jnp.mean(t * t, axis=-1, keepdims=True) + EPSILON)).astype(bf16)
 
-    chunks(rows, 16, normed)
-    greet(place.peers() + [place.core_peer, place.far_peer])
+    def scale(ref, gain, columns, into, at):
+        @pl.loop(0, RING)
+        def _(t):
+            for j, cols in enumerate(columns(t)):
+                part = (ref[:, cols].astype(f32) * gain).astype(bf16)
+                into[t, :, pl.ds(at + j * cols.size, cols.size)] = part
+
+    def prepare():
+        chunks(rows, 16, normed)
+        for copy in fetch[:3]:
+            copy.wait()
+        gain = column(gain_one[...].astype(f32))
+        scale(wq, gain, lambda t: [block_at(t, head)], heads, 0)
+        scale(wk, gain, lambda t: [block_at(t // groups, head)], heads, head)
+        scale(wv, gain, lambda t: [block_at(t // groups, head)], heads, 2 * head)
+
+    greet(place.peers() + [place.core_peer, place.far_peer], prepare)
     down_w = seq_gather(wdown, wdown_all, down_seq, place)
     x_blocks, dy_blocks = ByOwner(x_all, rows), ByArrival(dy_all, rows, place)
 
@@ -901,44 +926,18 @@
 
     out_w = out_flow()
 
-    def scale(ref, gain):
-        def body(cols):
-            ref[:, cols] = (ref[:, cols].astype(f32) * gain).astype(bf16)
-
-        chunks(ref.shape[1], 512, body)
-
-    for copy in fetch[:3]:
-        copy.wait()
-    gain = column(gain_one[...].astype(f32))
-    for ref in (wq, wk, wv):
-        scale(ref, gain)
-
-    def spread(pieces, dst, i, swap, seq, group=RING):
-        def to(c, into):
-            cols = pieces(c)
-            each = into.shape[1] // len(cols)
-            return [(src, into.at[:, pl.ds(j * each, each)]) for j, src in enumerate(cols)]
-
+    def spread(src, dst, swap, seq, sem, group=RING):
         rows_of_s = dst if seq is None else dst.at[place.s]
-        own = rows_of_s.at[place.c]
-        for src, into in to(place.c, own):
-            pltpu.make_async_copy(src, into, local.at[i]).start()
-        yield from exchange(lambda o: to(place.at(o), own), lambda o: rows_of_s.at[place.at(o)], swap, place, group)
-        pltpu.make_async_copy(own, own, local.at[i]).wait()
+        own = pltpu.make_async_copy(src.at[place.c], rows_of_s.at[place.c], sem)
+        own.start()
+        yield from by_owner(src, rows_of_s, swap, place, group)
+        own.wait()
         if seq is not None:
             yield from seq_gather(rows_of_s, dst, seq, place)
 
-    def head_columns(t):
-        kv = block_at(t // groups, head)
-        return [wq.at[:, block_at(t, head)], wk.at[:, kv], wv.at[:, kv]]
-
-    def unit_columns(ref):
-        own = wdown.shape[0]
-        return lambda t: [ref.at[:, block_at(i * RING + t, own)] for i in range(SEQ)]
-
-    qkv_w = spread(head_columns, wqkv_all, 3, qkv_swap, qkv_seq)
-    gate_w = spread(unit_columns(wg), wg_all, 4, gate_swap, gate_seq, 2)
-    up_w = spread(unit_columns(wu), wu_own, 5, up_swap, None, 2)
+    qkv_w = spread(heads, wqkv_all, qkv_swap, qkv_seq, local.at[3])
+    gate_w = spread(gate_units, wg_all, gate_swap, gate_seq, local.at[4], 2)
+    up_w = spread(up_units, wu_own, up_swap, None, local.at[5], 2)
     x_flow = grid_gather(xhat, x_blocks, x_grid, place)
     dy_flow = grid_gather(dy, dy_blocks, dy_grid, place)
     own_x = pltpu.make_async_copy(xhat, x_blocks.owner(place.c), local.at[6])
@@ -959,8 +958,9 @@
         for copy in fetch[3:]:
             copy.wait()
         gain = column(gain_two[...].astype(f32))
-        scale(wg, gain)
-        scale(wu, gain)
+        own = wdown.shape[0]
+        for ref, into in ((wg, gate_units), (wu, up_units)):
+            scale(ref, gain, lambda t: [block_at(i * RING + t, own) for i in range(SEQ)], into, 0)
 
     def find_rows():
         place_rows(
@@ -973,28 +973,32 @@
         for copy in load:
             copy.start()
 
-    def project_all():
-        for copy in load:
-            copy.wait()
-
-        def project(at):
-            qkv = dot(x_v[at, :], wqkv_v[...].reshape(width, 3 * head))
-            c, s = cos[at, :], sin[at, :]
-            q[at, :] = turned(qkv[:, :head], c, s, 1.0).astype(bf16)
-            k[at, :] = turned(qkv[:, head : 2 * head], c, s, 1.0).astype(bf16)
-            v[at, :] = qkv[:, 2 * head :].astype(bf16)
-
-        chunks(x_v.shape[0], 256, project)
-        for copy in saves:
-            copy.start()
-
-    def attend_all():
-        def attend(at):
-            prob = probabilities(q[at, :], k[...], pos_rows[at, :], start_rows[at, :], pos_cols[...])
-            ob[at, :] = dot(prob.astype(bf16), v[...]).astype(bf16)
-
-        chunks(x_v.shape[0], 256, attend)
-        ob_local[:, mine] = ob[block_at(place.c, rows), :]
+    halves = x_v.shape[0] // 2
+
+    def project(at):
+        qkv = dot(x_v[at, :], wqkv_v[...].reshape(width, 3 * head))
+        c, s = cos[at, :], sin[at, :]
+        q[at, :] = turned(qkv[:, :head], c, s, 1.0).astype(bf16)
+        k[at, :] = turned(qkv[:, head : 2 * head], c, s, 1.0).astype(bf16)
+        v[at, :] = qkv[:, 2 * head :].astype(bf16)
+
+    def project_half(i):
+        if i == 0:
+            for copy in load:
+                copy.wait()
+        chunks(halves, 256, lambda at: project(pl.ds(pl.multiple_of(i * halves + at.start, 256), 256)))
+        if i == 1:
+            for copy in saves:
+                copy.start()
+
+    def attend(at):
+        prob = probabilities(q[at, :], k[...], pos_rows[at, :], start_rows[at, :], pos_cols[...])
+        ob[at, :] = dot(prob.astype(bf16), v[...]).astype(bf16)
+
+    def attend_half(i):
+        chunks(halves, 256, lambda at: attend(pl.ds(pl.multiple_of(i * halves + at.start, 256), 256)))
+        if i == 1:
+            ob_local[:, mine] = ob[block_at(place.c, rows), :]
 
     def finish_hidden():
         load_out.wait()
@@ -1012,12 +1016,14 @@
         chunks(rows, 16, normed_two)
 
     works = {
-        "S": scale_units, "R": find_rows, "L": load_attention, "P": project_all,
-        "A": attend_all, "W": load_out.start, "H": finish_hidden,
+        "S": scale_units, "R": find_rows, "L": load_attention, "W": load_out.start, "H": finish_hidden,
     }
+    turns = {"P": iter((0, 1)), "A": iter((0, 1))}
     for step in plan:
         if step in flows:
             next(flows[step], None)
+        elif step in turns:
+            (project_half if step == "P" else attend_half)(next(turns[step]))
         else:
             works[step]()
     for name, flow in flows.items():
@@ -1190,18 +1196,18 @@
             pass
 
 
-def backward_kernel(plan, weighted, hidden, dy, x, q, k, v, ob_local, cos, sin, pos_rows, start_rows, pos_cols,
+def backward_kernel(plan, weighted, hidden, dy, x, pos_cols, q_hbm, k_hbm, v_hbm, ob_hbm, cos_hbm, sin_hbm, pos_hbm, start_hbm,
                     x_all, wqkv_all, wout_all, col,
-                    grad_x, out_grad, qkv_raw, gate_raw, up_raw, col_in,
+                    grad_x, out_grad, qkv_raw, gate_raw, up_raw, col_hbm,
+                    q, k, v, ob_local, cos, sin, pos_rows, start_rows,
                     x_v, wqkv_v, wout_v, branch, datt_own, datt, dqkv, dk, dv, sum_x, over_x, line_x,
-                    qkv_sent, qkv_near, qkv_far, qkv_in, out_sent, out_near, out_far, slots_o, local, *sems):
+                    qkv_sent, qkv_near, qkv_far, qkv_in, out_sent, out_near, out_far, slots_o, local, early, *sems):
     place = Place()
-    att_swap, col_swap, qkv_seq, qkv_swap, out_seq, out_ring = pairs_of(sems[:12])
-    x_grid = sems[12:]
+    att_swap, qkv_seq, qkv_swap, out_seq, out_ring = pairs_of(sems[:10])
+    x_grid, col_swap = sems[10:14], sems[14:]
     bf16, f32 = jnp.bfloat16, jnp.float32
     rows, width = x.shape
-    head = q.shape[1]
-    seq_len = q.shape[0]
+    seq_len, head = q.shape
     shard = out_grad.shape[0]
     loads = [
         pltpu.make_async_copy(src, dst, local.at[i])
@@ -1209,10 +1215,18 @@
     ]
     for copy in loads:
         copy.start()
-    col_blocks, qkv_blocks = Blocks(col, shard), Blocks(qkv_far, shard)
-    own_col = pltpu.make_async_copy(col_blocks[place.c], col_in.at[place.c], local.at[3])
-    own_col.start()
-    greet(place.peers() + [place.core_peer, place.far_peer])
+    qkv_blocks = Blocks(qkv_far, shard)
+    fetched = [
+        pltpu.make_async_copy(src, dst, early.at[i])
+        for i, (src, dst) in enumerate(
+            (
+                (ob_hbm, ob_local), (q_hbm, q), (k_hbm, k), (v_hbm, v),
+                (cos_hbm, cos), (sin_hbm, sin), (pos_hbm, pos_rows), (start_hbm, start_rows),
+            )
+        )
+    ]
+    for copy in fetched:
+        copy.start()
     def norm_back(tensor, grads):
         scale = lax.rsqrt(jnp.mean(tensor * tensor, axis=-1, keepdims=True) + EPSILON)
         inner = jnp.mean(grads * tensor, axis=-1, keepdims=True)
@@ -1223,9 +1237,11 @@
         grad_x[at, :] = grads
         branch[at, :] = grads.astype(bf16)
 
+    greet(place.peers() + [place.core_peer, place.far_peer], lambda: chunks(rows, 16, hidden_back))
+
     def heads_back():
-        chunks(rows, 16, hidden_back)
         loads[0].wait()
+        fetched[0].wait()
 
         def att_back(cols):
             datt_own[:, cols] = dot(branch[...], wout_v[cols, :], (1, 1)).astype(bf16)
@@ -1273,12 +1289,13 @@
         dk[...] = jnp.zeros_like(dk)
         dv[...] = jnp.zeros_like(dv)
         datt[mine, :] = datt_own[:, block_at(place.c, head)]
-        for copy in loads[1:]:
+        for copy in loads[1:] + fetched[1:]:
             copy.wait()
         chunks(seq_len, 256, attend_back)
         chunks(seq_len, 128, finish_back)
 
     part = wout_v.at[pl.ds(0, seq_len)]
+    col_in = wout_v.at[pl.ds(seq_len, RING * shard)]
     total = GridSum(part, over_x, line_x, x_grid, place)
 
     def part_x(i):
@@ -1293,14 +1310,21 @@
     unit = gate_raw.shape[1] // (RING * SEQ)
     groups = H // KVH
 
+    own_col = pltpu.make_async_copy(Blocks(col, shard)[place.c], Blocks(col_hbm, shard)[place.c], local.at[3])
+    own_col.start()
+    load_col = pltpu.make_async_copy(col_hbm, col_in, local.at[4])
+
+    def fetch_columns():
+        own_col.wait()
+        load_col.start()
+
     def move_columns():
-        own_col.wait()
+        load_col.wait()
         for c in range(RING):
             for side, raw in enumerate((gate_raw, up_raw)):
                 for i in range(SEQ):
-                    src = col_in.at[c, :, pl.ds((side * SEQ + i) * unit, unit)]
-                    into = raw.at[:, pl.ds((i * RING + c) * unit, unit)]
-                    pltpu.make_async_copy(src, into, local.at[4 + side]).start()
+                    value = col_in[pl.ds(c * shard, shard), pl.ds((side * SEQ + i) * unit, unit)]
+                    raw[:, pl.ds((i * RING + c) * unit, unit)] = value
 
     own_qkv = pltpu.make_async_copy(qkv_blocks[place.c], qkv_in.at[place.c], local.at[6])
 
@@ -1331,13 +1355,13 @@
     out_blocks = Owners(Blocks(out_far, shard), place)
     flows = {
         "a": att_flow,
-        "c": by_owner(col_blocks, col_in, col_swap, place, 2),
+        "c": by_owner(Blocks(col, shard), Blocks(col_hbm, shard), col_swap, place, 2),
         "o": ring_scatter(out_blocks, out_grad, slots_o, out_ring, place),
         "t": by_owner(qkv_blocks, qkv_in, qkv_swap, place),
     }
     works = {
         "h": heads_back, "B": all_back, "m": out_sum.across, "w": out_sum.own, "e": out_sum.last,
-        "M": qkv_sum.across, "W": qkv_sum.own, "E": qkv_last, "V": move_columns, "Z": tokens_back, "F": finish_qkv,
+        "M": qkv_sum.across, "W": qkv_sum.own, "E": qkv_last, "C": fetch_columns, "V": move_columns, "Z": tokens_back, "F": finish_qkv,
     }
     turns = {"n": each(out_sum.near, 2), "N": each(qkv_sum.near, 2), "p": each(part_x), "l": each(total.along, 3)}
     for step in plan:
@@ -1347,11 +1371,6 @@
             next(turns[step])()
         else:
             works[step]()
-    if "V" in plan:
-        for raw, sem in ((gate_raw, local.at[4]), (up_raw, local.at[5])):
-            pltpu.make_async_copy(raw, raw, sem).wait()
-    else:
-        own_col.wait()
     for name, flow in flows.items():
         if name in plan:
             for _ in flow:
@@ -1377,7 +1396,7 @@
 HBM = pl.ANY
 
 
-ATTENTION_PLAN = "dqxoooxoooxooRqqoooxxSggggqqLyPAbygggyuuuuyooWyybHdgu"
+ATTENTION_PLAN = "dqxoooxoooxooRqqoooxxSggggqqLyPPAAbygggyuuuuyooWyybHdgu"
 
 
 def attention_stage(
@@ -1431,6 +1450,9 @@
             VMEM(w_value.shape, bf16),
             VMEM(w_gate.shape, bf16),
             VMEM(w_up.shape, bf16),
+            VMEM((n, shard, 3 * head), bf16),
+            VMEM((n, shard, ff_mine), bf16),
+            VMEM((n, shard, ff_mine), bf16),
             VMEM((seq_len, width), bf16),
             VMEM((SEQ, n, shard, 3 * head), bf16),
             VMEM((SEQ, n, shard, width), bf16),
@@ -1480,12 +1502,12 @@
     )
 
 
-BACKWARD_PLAN = "channmacccBppNpNplMlwWclEtVZteooooFo"
+BACKWARD_PLAN = "hannmaccccBpNpNplMplwWlEtcCZVteoooooF"
 
 
 def backward_stage(args, columns, plan):
     bf16, f32, n, head = jnp.bfloat16, jnp.float32, RING, HDIM
-    (rows, width), seq_len, shard = args[0].shape, args[4].shape[0], columns[0]
+    (rows, width), seq_len, shard = args[0].shape, args[5].shape[0], columns[0]
     ff_mine = columns[1] // n
     piece = (n * shard, width)
     qkv_piece = (n * shard, 3 * head)
@@ -1497,12 +1519,16 @@
             shaped((shard, (H + 2 * KVH) * head), f32),
             shaped(columns),
             shaped(columns),
-            shaped((n, shard, 2 * ff_mine)),
+            shaped((n * shard, 2 * ff_mine)),
         ],
         args,
-        [VMEM] * 13 + [HBM] * 4,
-        [VMEM] * 3 + [HBM] * 3,
-        [
+        [VMEM] * 5 + [HBM] * 12,
+        [VMEM] * 5 + [HBM],
+        [VMEM((seq_len, head), bf16)] * 3
+        + [VMEM((rows, H * head), bf16)]
+        + [VMEM((seq_len, head // 2), f32)] * 2
+        + [VMEM((seq_len, 1), f32)] * 2
+        + [
             VMEM((seq_len, width), bf16),
             VMEM((width, 3 * head), bf16),
             VMEM((H * head, width), bf16),
@@ -1519,13 +1545,14 @@
         + [VMEM((2,) + qkv_piece, bf16), VMEM((2,) + qkv_piece, bf16), VMEM(qkv_piece, bf16)]
         + [VMEM((n, shard, 3 * head), bf16)]
         + [VMEM((2,) + piece, bf16), VMEM((2,) + piece, bf16), VMEM(piece, bf16)]
-        + [VMEM((2, n // 2, shard, width), bf16), DMA((7,))]
-        + pair_sems() * 2
+        + [VMEM((2, n // 2, shard, width), bf16), DMA((7,)), DMA((8,))]
+        + pair_sems()
         + seq_sems()
         + pair_sems()
         + seq_sems()
         + ring_sems()
-        + grid_sum_sems(),
+        + grid_sum_sems()
+        + pair_sems(),
         5,
     )
     return outs[:-1]
@@ -1558,8 +1585,8 @@
     output = (hidden + out_sum).astype(bf16)[None]
 
     grad_tokens, out_grad, qkv_raw, gate_raw, up_raw = backward_stage(
-        (dweighted, hidden, cotangent[0], tokens[0], q, k, v, ob_local)
-        + tuple(where)
+        (dweighted, hidden, cotangent[0], tokens[0], where[4], q, k, v, ob_local)
+        + tuple(where[:4])
         + (x_all, wqkv_all, wout_all, col_sum),
         w_gate.shape, BACKWARD_PLAN,
     )

time: 495 us -> 480 us (0.970)
  Pallas kernels: 478 us -> 466 us
    pallas_call x3, Pallas kernels: 478 us -> 466 us  [call(): pl.pallas_call(body, out_shape=outs, in_specs=[pl.BlockSpec(memory_space=...]
where the time goes in v1:
time: 480 us
  Pallas kernels  466 us (97%)
  other arithmetic  10.6 us (2%)
    pallas_call x3, Pallas kernels, call(): pl.pallas_call(body, out_shape=outs, in_specs=[pl.BlockSpec(memory_space=...  466 us

profile of v1, /device:TPU:0, one launch (start us, length us, event | category | flops | bytes accessed | tf_op | source)
XLA Modules:
  0.0 480.1 jit_solution(8494435105695671577)
XLA Ops:
  0.6 190.8 %shard_map.248 = (f32[128,2048]{1,0:T(8,128)}, bf16[128,2048]{1,0:T(8,128)(2,1)}, bf16[128,2048]{1,0:T(8,128)(2,1)}, f32[1024,128]{1,0:T(8,128)}, f32[1024,128]{...) custom-call(bf16[128,2048]{1,0:T(8,128)(2,1)} %bitcast.16, ...), custom_call_target="tpu_custom_call" | custom-call | tf_op jit(solution)/shard_map/pallas_call | solution.py:800
  191.5 140.1 %shard_map.249 = (f32[128,2048]{1,0:T(8,128)}, f32[128,2048]{1,0:T(8,128)}, bf16[512,2048]{1,0:T(8,128)(2,1)}, bf16[256,2048]{1,0:T(8,128)(2,1)}) custom-call(bf16[128,2048]{1,0:T(8,128)(2,1)} %get-tuple-element.39.hhat, bf16[1024,2048]{1,0:T(8,128)(2,1)} %get-tuple-element.40.dy_hbm, bf16[2048,1024]{1,0:T(8,128)(2,1)} %bitcast.13, ...), custom_call_target="tpu_custom_call" | custom-call | tf_op jit(solution)/shard_map/pallas_call | solution.py:800
  331.6 0.0 copy-start.9
  331.6 135.4 %shard_map.250 = (f32[128,2048]{1,0:T(8,128)}, f32[64,2048]{1,0:T(8,128)}, f32[64,4096]{1,0:T(8,128)}, bf16[64,8192]{1,0:T(8,128)(2,1)}, bf16[64,8192]{1,0:T(8,128)(2,1)}, /*index=5*/bf16[512,2048]{1,0:T(8,128)(2,1)}) custom-call(f32[128,2048]{1,0:T(8,128)} %get-tuple-element.45.weighted, f32[128,2048]{1,0:T(8,128)} %get-tuple-element.38.hidden, ...), custom_call_target="tpu_custom_call" | custom-call | tf_op jit(solution)/shard_map/pallas_call | solution.py:800
  467.1 0.0 copy-done.9
  467.1 0.0 copy-start.10
  467.1 0.0 copy-start.4
  467.1 0.0 copy-start.7
  467.1 0.0 copy-start.8
  467.2 0.0 copy-start.5
  467.2 5.1 %convert_multiply_fusion = (f32[64,8192]{1,0:T(8,128)}, f32[64]{0:T(128)S(1)}, f32[64]{0:T(128)S(1)}, f32[64,8192]{1,0:T(8,128)}) fusion(bf16[64,8192]{1,0:T(8,128)(2,1)} %get-tuple-element.63, f32[64]{0:T(128)S(1)} %convert_element_type.44, bf16[64,8192]{1,0:T(8,128)(2,1)} %w_up.1, bf16[64,8192]{1,0:T(8,128)(2,1)} %w_gate.1, bf16[64,8192]{1,0:T(8,128)(2,1)} %get-tuple-element.62), kind=kLoop, calls=%fused_computation | loop fusion | flops 5242752 | bytes 8389376 | tf_op jit(solution)/shard_map/mul | solution.py:1614
  472.3 0.0 copy-start.1
  472.3 0.5 add.15
  472.8 0.0 copy-done.10
  472.8 0.0 copy-done.4
  472.8 0.0 copy-done.7
  472.8 0.0 copy-done.8
  472.9 1.0 slice_multiply_fusion.1
  473.8 0.0 copy-done.5
  473.9 0.0 copy-start
  473.9 0.0 copy-start.2
  473.9 1.0 slice_multiply_fusion
  474.9 0.5 add_add_fusion
  475.4 0.0 copy-done.1
  475.4 1.6 convert_element_type.45
  477.0 0.0 copy-start.3
  477.0 0.0 copy-done
  477.0 0.0 copy-done.2
  477.0 0.0 copy-start.6
  477.0 0.9 fusion.2
  477.9 0.5 copy-done.3
  478.4 1.0 copy.30
  479.4 0.0 copy-done.6
  479.4 0.8 copy.31
  (2 shorter events, 0.0 us)
Async XLA Ops:
  331.6 135.5 %copy-start.9 = (bf16[64]{0:T(256)(128)(2,1)S(1)}, bf16[64]{0:T(256)(128)(2,1)}, u32[]{:S(2)}) copy-start(bf16[64]{0:T(256)(128)(2,1)} %param.24) | copy-start | bytes 388
  467.1 5.7 %copy-start.10 = (bf16[64]{0:T(256)(128)(2,1)S(1)}, bf16[64]{0:T(256)(128)(2,1)}, u32[]{:S(2)}) copy-start(bf16[64]{0:T(256)(128)(2,1)} %param.19) | copy-start | bytes 388
  467.1 5.7 %copy-start.4 = (f32[64,4096]{1,0:T(8,128)S(1)}, f32[64,4096]{1,0:T(8,128)}, u32[]{:S(2)}) copy-start(f32[64,4096]{1,0:T(8,128)} %get-tuple-element.60) | copy-start | bytes 3145732
  467.1 5.7 %copy-start.7 = (bf16[64,1024]{1,0:T(8,128)(2,1)S(1)}, bf16[64,1024]{1,0:T(8,128)(2,1)}, u32[]{:S(2)}) copy-start(bf16[64,1024]{1,0:T(8,128)(2,1)} %w_key.1) | copy-start | bytes 393220
  467.1 5.7 %copy-start.8 = (bf16[64,1024]{1,0:T(8,128)(2,1)S(1)}, bf16[64,1024]{1,0:T(8,128)(2,1)}, u32[]{:S(2)}) copy-start(bf16[64,1024]{1,0:T(8,128)(2,1)} %w_value.1) | copy-start | bytes 393220
  467.2 6.7 %copy-start.5 = (bf16[64,2048]{1,0:T(8,128)(2,1)S(1)}, bf16[64,2048]{1,0:T(8,128)(2,1)}, u32[]{:S(2)}) copy-start(bf16[64,2048]{1,0:T(8,128)(2,1)} %w_query.1) | copy-start | bytes 786436
  472.3 3.1 copy-start.1
  473.9 3.1 copy-start
  473.9 3.1 copy-start.2
  477.0 1.4 copy-start.3
  477.0 2.4 copy-start.6

commit v2 on v1

--- a/solution.py
+++ b/solution.py
@@ -873,7 +873,7 @@
                      dy, w_query, w_key, w_value, wout, w_gate, w_up, wdown,
                      hidden, hhat, ob_local, cos, sin, pos_rows, start_rows, pos_cols,
                      q_out, k_out, v_out, x_all, dy_all, wqkv_all, wout_all, wg_all, wu_own, wdown_all,
-                     xhat, wq, wk, wv, wg, wu, heads, gate_units, up_units, x_v, wqkv_v, wout_v, q, k, v, ob, local, loads, *sems):
+                     xhat, wq, wk, wv, wg, wu, wout_s, wdown_s, dy_s, heads, gate_units, up_units, x_v, wqkv_v, wout_v, q, k, v, ob, local, loads, *sems):
     place = Place()
     qkv_swap, qkv_seq, out_ring, out_seq, ob_swap, gate_swap, gate_seq, up_swap, down_seq = pairs_of(sems[:18])
     x_grid, dy_grid = sems[18:22], sems[22:26]
@@ -883,17 +883,20 @@
     groups = H // KVH
     fetch = [
         pltpu.make_async_copy(src, dst, loads.at[i])
-        for i, (src, dst) in enumerate(((w_query, wq), (w_key, wk), (w_value, wv), (w_gate, wg), (w_up, wu)))
+        for i, (src, dst) in enumerate(
+            (
+                (w_query, wq), (w_key, wk), (w_value, wv), (w_gate, wg), (w_up, wu),
+                (wout, wout_s), (wdown, wdown_s), (dy, dy_s),
+            )
+        )
     ]
     for copy in fetch:
         copy.start()
     keep = [
-        pltpu.make_async_copy(wout, wout_all.at[place.s, place.c], local.at[0]),
-        pltpu.make_async_copy(wdown, wdown_all.at[place.s], local.at[1]),
-        pltpu.make_async_copy(dy, ByArrival(dy_all, rows, place).owner(place.c), local.at[2]),
+        pltpu.make_async_copy(wout_s, wout_all.at[place.s, place.c], local.at[0]),
+        pltpu.make_async_copy(wdown_s, wdown_all.at[place.s], local.at[1]),
+        pltpu.make_async_copy(dy_s, ByArrival(dy_all, rows, place).owner(place.c), local.at[2]),
     ]
-    for copy in keep:
-        copy.start()
 
     def normed(at):
         t = x[at, :].astype(f32)
@@ -908,6 +911,9 @@
 
     def prepare():
         chunks(rows, 16, normed)
+        for loaded, kept in zip(fetch[5:], keep):
+            loaded.wait()
+            kept.start()
         for copy in fetch[:3]:
             copy.wait()
         gain = column(gain_one[...].astype(f32))
@@ -955,7 +961,7 @@
     load_out = pltpu.make_async_copy(wout_all, wout_v, local.at[0])
 
     def scale_units():
-        for copy in fetch[3:]:
+        for copy in fetch[3:5]:
             copy.wait()
         gain = column(gain_two[...].astype(f32))
         own = wdown.shape[0]
@@ -1037,7 +1043,7 @@
         for copy in load:
             copy.wait()
     if "S" not in plan:
-        for copy in fetch[3:]:
+        for copy in fetch[3:5]:
             copy.wait()
     if "o" not in plan:
         keep[0].wait()
@@ -1310,27 +1316,23 @@
     unit = gate_raw.shape[1] // (RING * SEQ)
     groups = H // KVH
 
-    own_col = pltpu.make_async_copy(Blocks(col, shard)[place.c], Blocks(col_hbm, shard)[place.c], local.at[3])
-    own_col.start()
-    load_col = pltpu.make_async_copy(col_hbm, col_in, local.at[4])
-
     def fetch_columns():
-        own_col.wait()
-        load_col.start()
+        for k in (0,) + OFFSETS:
+            c = place.at(k)
+            source = Blocks(col_hbm if k else col, shard)
+            pltpu.make_async_copy(source[c], Blocks(col_in, shard)[c], local.at[4]).start()
 
     def move_columns():
-        load_col.wait()
+        pltpu.make_async_copy(col_in, col_in, local.at[4]).wait()
         for c in range(RING):
             for side, raw in enumerate((gate_raw, up_raw)):
                 for i in range(SEQ):
                     value = col_in[pl.ds(c * shard, shard), pl.ds((side * SEQ + i) * unit, unit)]
                     raw[:, pl.ds((i * RING + c) * unit, unit)] = value
 
-    own_qkv = pltpu.make_async_copy(qkv_blocks[place.c], qkv_in.at[place.c], local.at[6])
-
     def qkv_last():
         qkv_sum.last()
-        own_qkv.start()
+        qkv_in[place.c] = qkv_blocks[place.c][...]
 
     def tokens_back():
         total.last(sum_x)
@@ -1341,7 +1343,6 @@
         chunks(rows, 16, token_back)
 
     def finish_qkv():
-        own_qkv.wait()
         for t in range(H):
             qkv_raw[:, pl.ds(t * head, head)] = qkv_in[t, :, pl.ds(0, head)].astype(f32)
         for side in (1, 2):
@@ -1396,7 +1397,7 @@
 HBM = pl.ANY
 
 
-ATTENTION_PLAN = "dqxoooxoooxooRqqoooxxSggggqqLyPPAAbygggyuuuuyooWyybHdgu"
+ATTENTION_PLAN = "doooooooooooxxqxxqqRSggggqqxLyPPAAbgygyuuuuyoogWbHydgu"
 
 
 def attention_stage(
@@ -1450,6 +1451,9 @@
             VMEM(w_value.shape, bf16),
             VMEM(w_gate.shape, bf16),
             VMEM(w_up.shape, bf16),
+            VMEM(w_out.shape, bf16),
+            VMEM(w_down.shape, bf16),
+            VMEM((rows, width), bf16),
             VMEM((n, shard, 3 * head), bf16),
             VMEM((n, shard, ff_mine), bf16),
             VMEM((n, shard, ff_mine), bf16),
@@ -1458,7 +1462,7 @@
             VMEM((SEQ, n, shard, width), bf16),
         ]
         + [VMEM((seq_len, head), bf16)] * 4
-        + [DMA((7,)), DMA((5,))]
+        + [DMA((7,)), DMA((8,))]
         + pair_sems()
         + seq_sems()
         + ring_sems()

time: 480 us -> 465 us (0.969)
  Pallas kernels: 466 us -> 451 us
    pallas_call x3, Pallas kernels: 466 us -> 451 us  [call(): pl.pallas_call(body, out_shape=outs, in_specs=[pl.BlockSpec(memory_space=...]
where the time goes in v2:
time: 465 us
  Pallas kernels  451 us (97%)
  other arithmetic  10.6 us (2%)
    pallas_call x3, Pallas kernels, call(): pl.pallas_call(body, out_shape=outs, in_specs=[pl.BlockSpec(memory_space=...  451 us

profile of v2, /device:TPU:0, one launch (start us, length us, event | category | flops | bytes accessed | tf_op | source)
XLA Modules:
  0.0 464.9 jit_solution(3658378676062735909)
XLA Ops:
  0.6 179.4 %shard_map.248 = (f32[128,2048]{1,0:T(8,128)}, bf16[128,2048]{1,0:T(8,128)(2,1)}, bf16[128,2048]{1,0:T(8,128)(2,1)}, f32[1024,128]{1,0:T(8,128)}, f32[1024,128]{...) custom-call(bf16[128,2048]{1,0:T(8,128)(2,1)} %bitcast.16, ...), custom_call_target="tpu_custom_call" | custom-call | tf_op jit(solution)/shard_map/pallas_call | solution.py:800
  180.0 137.2 %shard_map.249 = (f32[128,2048]{1,0:T(8,128)}, f32[128,2048]{1,0:T(8,128)}, bf16[512,2048]{1,0:T(8,128)(2,1)}, bf16[256,2048]{1,0:T(8,128)(2,1)}) custom-call(bf16[128,2048]{1,0:T(8,128)(2,1)} %get-tuple-element.39.hhat, bf16[1024,2048]{1,0:T(8,128)(2,1)} %get-tuple-element.40.dy_hbm, bf16[2048,1024]{1,0:T(8,128)(2,1)} %bitcast.13, ...), custom_call_target="tpu_custom_call" | custom-call | tf_op jit(solution)/shard_map/pallas_call | solution.py:800
  317.2 0.0 copy-start.9
  317.2 134.6 %shard_map.250 = (f32[128,2048]{1,0:T(8,128)}, f32[64,2048]{1,0:T(8,128)}, f32[64,4096]{1,0:T(8,128)}, bf16[64,8192]{1,0:T(8,128)(2,1)}, bf16[64,8192]{1,0:T(8,128)(2,1)}, /*index=5*/bf16[512,2048]{1,0:T(8,128)(2,1)}) custom-call(f32[128,2048]{1,0:T(8,128)} %get-tuple-element.45.weighted, f32[128,2048]{1,0:T(8,128)} %get-tuple-element.38.hidden, ...), custom_call_target="tpu_custom_call" | custom-call | tf_op jit(solution)/shard_map/pallas_call | solution.py:800
  451.8 0.0 copy-done.9
  451.8 0.0 copy-start.10
  451.9 0.0 copy-start.4
  451.9 0.0 copy-start.7
  451.9 0.0 copy-start.8
  451.9 0.0 copy-start.5
  451.9 5.1 %convert_multiply_fusion = (f32[64,8192]{1,0:T(8,128)}, f32[64]{0:T(128)S(1)}, f32[64]{0:T(128)S(1)}, f32[64,8192]{1,0:T(8,128)}) fusion(bf16[64,8192]{1,0:T(8,128)(2,1)} %get-tuple-element.63, f32[64]{0:T(128)S(1)} %convert_element_type.44, bf16[64,8192]{1,0:T(8,128)(2,1)} %w_up.1, bf16[64,8192]{1,0:T(8,128)(2,1)} %w_gate.1, bf16[64,8192]{1,0:T(8,128)(2,1)} %get-tuple-element.62), kind=kLoop, calls=%fused_computation | loop fusion | flops 5242752 | bytes 8389376 | tf_op jit(solution)/shard_map/mul | solution.py:1618
  457.0 0.0 copy-start.1
  457.1 0.5 add.15
  457.6 0.0 copy-done.10
  457.6 0.0 copy-done.4
  457.6 0.0 copy-done.7
  457.6 0.0 copy-done.8
  457.6 1.0 slice_multiply_fusion.1
  458.6 0.0 copy-done.5
  458.6 0.0 copy-start
  458.6 0.0 copy-start.2
  458.6 1.0 slice_multiply_fusion
  459.6 0.5 add_add_fusion
  460.1 0.0 copy-done.1
  460.1 1.6 convert_element_type.45
  461.7 0.0 copy-start.3
  461.7 0.0 copy-done
  461.7 0.0 copy-done.2
  461.7 0.0 copy-start.6
  461.7 0.9 fusion.2
  462.6 0.5 copy-done.3
  463.1 1.0 copy.30
  464.1 0.0 copy-done.6
  464.1 0.8 copy.31
  (2 shorter events, 0.0 us)
Async XLA Ops:
  317.2 134.6 %copy-start.9 = (bf16[64]{0:T(256)(128)(2,1)S(1)}, bf16[64]{0:T(256)(128)(2,1)}, u32[]{:S(2)}) copy-start(bf16[64]{0:T(256)(128)(2,1)} %param.24) | copy-start | bytes 388
  451.8 5.7 %copy-start.10 = (bf16[64]{0:T(256)(128)(2,1)S(1)}, bf16[64]{0:T(256)(128)(2,1)}, u32[]{:S(2)}) copy-start(bf16[64]{0:T(256)(128)(2,1)} %param.19) | copy-start | bytes 388
  451.9 5.7 %copy-start.4 = (f32[64,4096]{1,0:T(8,128)S(1)}, f32[64,4096]{1,0:T(8,128)}, u32[]{:S(2)}) copy-start(f32[64,4096]{1,0:T(8,128)} %get-tuple-element.60) | copy-start | bytes 3145732
  451.9 5.7 %copy-start.7 = (bf16[64,1024]{1,0:T(8,128)(2,1)S(1)}, bf16[64,1024]{1,0:T(8,128)(2,1)}, u32[]{:S(2)}) copy-start(bf16[64,1024]{1,0:T(8,128)(2,1)} %w_key.1) | copy-start | bytes 393220
  451.9 5.7 %copy-start.8 = (bf16[64,1024]{1,0:T(8,128)(2,1)S(1)}, bf16[64,1024]{1,0:T(8,128)(2,1)}, u32[]{:S(2)}) copy-start(bf16[64,1024]{1,0:T(8,128)(2,1)} %w_value.1) | copy-start | bytes 393220
  451.9 6.7 %copy-start.5 = (bf16[64,2048]{1,0:T(8,128)(2,1)S(1)}, bf16[64,2048]{1,0:T(8,128)(2,1)}, u32[]{:S(2)}) copy-start(bf16[64,2048]{1,0:T(8,128)(2,1)} %w_query.1) | copy-start | bytes 786436
  457.0 3.1 copy-start.1
  458.6 3.1 copy-start
  458.6 3.1 copy-start.2
  461.7 1.4 copy-start.3
  461.7 2.4 copy-start.6

commit v3 on v2

--- a/solution.py
+++ b/solution.py
@@ -1506,7 +1506,7 @@
     )
 
 
-BACKWARD_PLAN = "hannmaccccBpNpNplMplwWlEtcCZVteoooooF"
+BACKWARD_PLAN = "hannmaccccBpNpNplMplwWlEteoZocCoVtooF"
 
 
 def backward_stage(args, columns, plan):

time: 465 us -> 464 us (level)
  no operation moved by 1% of the time
where the time goes in v3:
time: 464 us
  Pallas kernels  450 us (97%)
  other arithmetic  10.6 us (2%)
    pallas_call x3, Pallas kernels, call(): pl.pallas_call(body, out_shape=outs, in_specs=[pl.BlockSpec(memory_space=...  450 us

profile of v3, /device:TPU:0, one launch (start us, length us, event | category | flops | bytes accessed | tf_op | source)
XLA Modules:
  0.0 464.0 jit_solution(6340533097897653090)
XLA Ops:
  0.6 179.4 %shard_map.248 = (f32[128,2048]{1,0:T(8,128)}, bf16[128,2048]{1,0:T(8,128)(2,1)}, bf16[128,2048]{1,0:T(8,128)(2,1)}, f32[1024,128]{1,0:T(8,128)}, f32[1024,128]{...) custom-call(bf16[128,2048]{1,0:T(8,128)(2,1)} %bitcast.16, ...), custom_call_target="tpu_custom_call" | custom-call | tf_op jit(solution)/shard_map/pallas_call | solution.py:800
  180.0 137.2 %shard_map.249 = (f32[128,2048]{1,0:T(8,128)}, f32[128,2048]{1,0:T(8,128)}, bf16[512,2048]{1,0:T(8,128)(2,1)}, bf16[256,2048]{1,0:T(8,128)(2,1)}) custom-call(bf16[128,2048]{1,0:T(8,128)(2,1)} %get-tuple-element.39.hhat, bf16[1024,2048]{1,0:T(8,128)(2,1)} %get-tuple-element.40.dy_hbm, bf16[2048,1024]{1,0:T(8,128)(2,1)} %bitcast.13, ...), custom_call_target="tpu_custom_call" | custom-call | tf_op jit(solution)/shard_map/pallas_call | solution.py:800
  317.2 0.0 copy-start.9
  317.2 133.7 %shard_map.250 = (f32[128,2048]{1,0:T(8,128)}, f32[64,2048]{1,0:T(8,128)}, f32[64,4096]{1,0:T(8,128)}, bf16[64,8192]{1,0:T(8,128)(2,1)}, bf16[64,8192]{1,0:T(8,128)(2,1)}, /*index=5*/bf16[512,2048]{1,0:T(8,128)(2,1)}) custom-call(f32[128,2048]{1,0:T(8,128)} %get-tuple-element.45.weighted, f32[128,2048]{1,0:T(8,128)} %get-tuple-element.38.hidden, ...), custom_call_target="tpu_custom_call" | custom-call | tf_op jit(solution)/shard_map/pallas_call | solution.py:800
  450.9 0.0 copy-done.9
  450.9 0.0 copy-start.10
  450.9 0.0 copy-start.4
  450.9 0.0 copy-start.7
  451.0 0.0 copy-start.8
  451.0 0.0 copy-start.5
  451.0 5.1 %convert_multiply_fusion = (f32[64,8192]{1,0:T(8,128)}, f32[64]{0:T(128)S(1)}, f32[64]{0:T(128)S(1)}, f32[64,8192]{1,0:T(8,128)}) fusion(bf16[64,8192]{1,0:T(8,128)(2,1)} %get-tuple-element.63, f32[64]{0:T(128)S(1)} %convert_element_type.44, bf16[64,8192]{1,0:T(8,128)(2,1)} %w_up.1, bf16[64,8192]{1,0:T(8,128)(2,1)} %w_gate.1, bf16[64,8192]{1,0:T(8,128)(2,1)} %get-tuple-element.62), kind=kLoop, calls=%fused_computation | loop fusion | flops 5242752 | bytes 8389376 | tf_op jit(solution)/shard_map/mul | solution.py:1618
  456.1 0.0 copy-start.1
  456.1 0.5 add.15
  456.6 0.0 copy-done.10
  456.7 0.0 copy-done.4
  456.7 0.0 copy-done.7
  456.7 0.0 copy-done.8
  456.7 1.0 slice_multiply_fusion.1
  457.7 0.0 copy-done.5
  457.7 0.0 copy-start
  457.7 0.0 copy-start.2
  457.7 1.0 slice_multiply_fusion
  458.7 0.5 add_add_fusion
  459.2 0.0 copy-done.1
  459.2 1.6 convert_element_type.45
  460.8 0.0 copy-start.3
  460.8 0.0 copy-done
  460.8 0.0 copy-done.2
  460.8 0.0 copy-start.6
  460.8 0.9 fusion.2
  461.7 0.5 copy-done.3
  462.2 1.0 copy.30
  463.2 0.0 copy-done.6
  463.2 0.8 copy.31
  (2 shorter events, 0.0 us)
Async XLA Ops:
  317.2 133.7 %copy-start.9 = (bf16[64]{0:T(256)(128)(2,1)S(1)}, bf16[64]{0:T(256)(128)(2,1)}, u32[]{:S(2)}) copy-start(bf16[64]{0:T(256)(128)(2,1)} %param.24) | copy-start | bytes 388
  450.9 5.7 %copy-start.10 = (bf16[64]{0:T(256)(128)(2,1)S(1)}, bf16[64]{0:T(256)(128)(2,1)}, u32[]{:S(2)}) copy-start(bf16[64]{0:T(256)(128)(2,1)} %param.19) | copy-start | bytes 388
  450.9 5.7 %copy-start.4 = (f32[64,4096]{1,0:T(8,128)S(1)}, f32[64,4096]{1,0:T(8,128)}, u32[]{:S(2)}) copy-start(f32[64,4096]{1,0:T(8,128)} %get-tuple-element.60) | copy-start | bytes 3145732
  450.9 5.7 %copy-start.7 = (bf16[64,1024]{1,0:T(8,128)(2,1)S(1)}, bf16[64,1024]{1,0:T(8,128)(2,1)}, u32[]{:S(2)}) copy-start(bf16[64,1024]{1,0:T(8,128)(2,1)} %w_key.1) | copy-start | bytes 393220
  451.0 5.7 %copy-start.8 = (bf16[64,1024]{1,0:T(8,128)(2,1)S(1)}, bf16[64,1024]{1,0:T(8,128)(2,1)}, u32[]{:S(2)}) copy-start(bf16[64,1024]{1,0:T(8,128)(2,1)} %w_value.1) | copy-start | bytes 393220
  451.0 6.7 %copy-start.5 = (bf16[64,2048]{1,0:T(8,128)(2,1)S(1)}, bf16[64,2048]{1,0:T(8,128)(2,1)}, u32[]{:S(2)}) copy-start(bf16[64,2048]{1,0:T(8,128)(2,1)} %w_query.1) | copy-start | bytes 786436
  456.1 3.1 copy-start.1
  457.7 3.1 copy-start
  457.7 3.1 copy-start.2
  460.8 1.4 copy-start.3
  460.8 2.4 copy-start.6

commit v4 on v3

--- a/solution.py
+++ b/solution.py
@@ -1095,7 +1095,7 @@
         def body(cols):
             dst[:, cols] = (dot(dgate[at, :], wg[cols, :], (1, 1)) + dot(dup[at, :], wu[cols, :], (1, 1))).astype(bf16)
 
-        chunks(width, 512, body)
+        chunks(width, 1024, body)
 
     def part_o(start, count, dst):
         at = pl.ds(start, count)

time: 464 us -> 463 us (level)
  no operation moved by 1% of the time
where the time goes in v4:
time: 463 us
  Pallas kernels  449 us (97%)
  other arithmetic  10.6 us (2%)
    pallas_call x3, Pallas kernels, call(): pl.pallas_call(body, out_shape=outs, in_specs=[pl.BlockSpec(memory_space=...  449 us

profile of v4, /device:TPU:0, one launch (start us, length us, event | category | flops | bytes accessed | tf_op | source)
XLA Modules:
  0.0 463.0 jit_solution(13998055975903724714)
XLA Ops:
  0.6 179.4 %shard_map.248 = (f32[128,2048]{1,0:T(8,128)}, bf16[128,2048]{1,0:T(8,128)(2,1)}, bf16[128,2048]{1,0:T(8,128)(2,1)}, f32[1024,128]{1,0:T(8,128)}, f32[1024,128]{...) custom-call(bf16[128,2048]{1,0:T(8,128)(2,1)} %bitcast.16, ...), custom_call_target="tpu_custom_call" | custom-call | tf_op jit(solution)/shard_map/pallas_call | solution.py:800
  180.0 136.8 %shard_map.249 = (f32[128,2048]{1,0:T(8,128)}, f32[128,2048]{1,0:T(8,128)}, bf16[512,2048]{1,0:T(8,128)(2,1)}, bf16[256,2048]{1,0:T(8,128)(2,1)}) custom-call(bf16[128,2048]{1,0:T(8,128)(2,1)} %get-tuple-element.39.hhat, bf16[1024,2048]{1,0:T(8,128)(2,1)} %get-tuple-element.40.dy_hbm, bf16[2048,1024]{1,0:T(8,128)(2,1)} %bitcast.13, ...), custom_call_target="tpu_custom_call" | custom-call | tf_op jit(solution)/shard_map/pallas_call | solution.py:800
  316.9 0.0 copy-start.9
  316.9 133.0 %shard_map.250 = (f32[128,2048]{1,0:T(8,128)}, f32[64,2048]{1,0:T(8,128)}, f32[64,4096]{1,0:T(8,128)}, bf16[64,8192]{1,0:T(8,128)(2,1)}, bf16[64,8192]{1,0:T(8,128)(2,1)}, /*index=5*/bf16[512,2048]{1,0:T(8,128)(2,1)}) custom-call(f32[128,2048]{1,0:T(8,128)} %get-tuple-element.45.weighted, f32[128,2048]{1,0:T(8,128)} %get-tuple-element.38.hidden, ...), custom_call_target="tpu_custom_call" | custom-call | tf_op jit(solution)/shard_map/pallas_call | solution.py:800
  449.9 0.0 copy-done.9
  449.9 0.0 copy-start.10
  449.9 0.0 copy-start.4
  449.9 0.0 copy-start.7
  449.9 0.0 copy-start.8
  450.0 0.0 copy-start.5
  450.0 5.1 %convert_multiply_fusion = (f32[64,8192]{1,0:T(8,128)}, f32[64]{0:T(128)S(1)}, f32[64]{0:T(128)S(1)}, f32[64,8192]{1,0:T(8,128)}) fusion(bf16[64,8192]{1,0:T(8,128)(2,1)} %get-tuple-element.63, f32[64]{0:T(128)S(1)} %convert_element_type.44, bf16[64,8192]{1,0:T(8,128)(2,1)} %w_up.1, bf16[64,8192]{1,0:T(8,128)(2,1)} %w_gate.1, bf16[64,8192]{1,0:T(8,128)(2,1)} %get-tuple-element.62), kind=kLoop, calls=%fused_computation | loop fusion | flops 5242752 | bytes 8389376 | tf_op jit(solution)/shard_map/mul | solution.py:1618
  455.1 0.0 copy-start.1
  455.1 0.5 add.15
  455.6 0.0 copy-done.10
  455.6 0.0 copy-done.4
  455.6 0.0 copy-done.7
  455.6 0.0 copy-done.8
  455.7 1.0 slice_multiply_fusion.1
  456.7 0.0 copy-done.5
  456.7 0.0 copy-start
  456.7 0.0 copy-start.2
  456.7 1.0 slice_multiply_fusion
  457.7 0.5 add_add_fusion
  458.2 0.0 copy-done.1
  458.2 1.6 convert_element_type.45
  459.8 0.0 copy-start.3
  459.8 0.0 copy-done
  459.8 0.0 copy-done.2
  459.8 0.0 copy-start.6
  459.8 0.9 fusion.2
  460.7 0.5 copy-done.3
  461.2 1.0 copy.30
  462.2 0.0 copy-done.6
  462.2 0.8 copy.31
  (2 shorter events, 0.0 us)
Async XLA Ops:
  316.9 133.0 %copy-start.9 = (bf16[64]{0:T(256)(128)(2,1)S(1)}, bf16[64]{0:T(256)(128)(2,1)}, u32[]{:S(2)}) copy-start(bf16[64]{0:T(256)(128)(2,1)} %param.24) | copy-start | bytes 388
  449.9 5.7 %copy-start.10 = (bf16[64]{0:T(256)(128)(2,1)S(1)}, bf16[64]{0:T(256)(128)(2,1)}, u32[]{:S(2)}) copy-start(bf16[64]{0:T(256)(128)(2,1)} %param.19) | copy-start | bytes 388
  449.9 5.7 %copy-start.4 = (f32[64,4096]{1,0:T(8,128)S(1)}, f32[64,4096]{1,0:T(8,128)}, u32[]{:S(2)}) copy-start(f32[64,4096]{1,0:T(8,128)} %get-tuple-element.60) | copy-start | bytes 3145732
  449.9 5.7 %copy-start.7 = (bf16[64,1024]{1,0:T(8,128)(2,1)S(1)}, bf16[64,1024]{1,0:T(8,128)(2,1)}, u32[]{:S(2)}) copy-start(bf16[64,1024]{1,0:T(8,128)(2,1)} %w_key.1) | copy-start | bytes 393220
  449.9 5.7 %copy-start.8 = (bf16[64,1024]{1,0:T(8,128)(2,1)S(1)}, bf16[64,1024]{1,0:T(8,128)(2,1)}, u32[]{:S(2)}) copy-start(bf16[64,1024]{1,0:T(8,128)(2,1)} %w_value.1) | copy-start | bytes 393220
  450.0 6.7 %copy-start.5 = (bf16[64,2048]{1,0:T(8,128)(2,1)S(1)}, bf16[64,2048]{1,0:T(8,128)(2,1)}, u32[]{:S(2)}) copy-start(bf16[64,2048]{1,0:T(8,128)(2,1)} %w_query.1) | copy-start | bytes 786436
  455.1 3.1 copy-start.1
  456.7 3.1 copy-start
  456.7 3.1 copy-start.2
  459.8 1.4 copy-start.3
  459.8 2.4 copy-start.6
